TPU v7x, 32 devices: a whole 2x2x4 slice. The times are simulated.
32 devices in a mesh: wide: 16 (over z, x, core), narrow: 2 (over y).
Axes of the slice: x: 2, y: 2, z: 4, core: 2. Of those that a mesh axis runs over, the one named last changes fastest.
Arguments:
- amplitudes: float32 [48, 1024, 1024], P('wide', None, 'narrow'), may hold values from -24 to 24
- integrals: float32 [16, 16, 1024, 1024], P('narrow', None, 'wide'), may hold values from -0.005859375 to 0.005859375
- pair_index: int32 [48, 2], P('wide'), may hold values from 0 to 199
- window_virtuals: int32 [16], replicated, may hold values from 0 to 1023
- occ_energy: float32 [200], replicated, may hold values from -3 to -0.5
- virt_energy: float32 [1024], replicated, may hold values from 0.3 to 6
Outputs:
- update: float32 [16, 16, 48], P('narrow', None, 'wide')
All inputs are finite; a program needn't handle non-finite values.
Results may differ from a plain program's by a relative error of at most 0.00013.
Values sent between devices are 32-bit elements; how exact they have to be, the bound alone decides.
No kernel may reach another device: no remote copies, remote signals or barrier semaphores. Data moves between devices by JAX's collectives and lax.ppermute only.
A program may use at most 128 MiB of HBM per device.

v0:
```python
import jax
import jax.numpy as jnp
from jax import lax
from jax.sharding import PartitionSpec as P


def lookup(table, indices):
    matches = (indices[..., None] == jnp.arange(table.shape[0], dtype=jnp.int32)).astype(
        jnp.float32
    )
    return jnp.sum(matches * table, axis=-1)


def contract(left_rows, right_rows):
    return lax.dot_general(
        left_rows.reshape(left_rows.shape[0], -1),
        right_rows.reshape(right_rows.shape[0], -1),
        (((1,), (1,)), ((), ())),
        precision=lax.Precision.HIGHEST,
        preferred_element_type=jnp.float32,
    )


def shards(amplitudes, integrals, pair_index, window_virtuals, occ_energy, virt_energy):
    exchanged = lax.all_to_all(amplitudes, "wide", split_axis=1, concat_axis=0, tiled=True)
    rows_here = integrals.shape[0]
    window = integrals.shape[1]
    first_block = integrals.shape[2]
    all_pairs = exchanged.shape[0]
    integral_rows = integrals.reshape(rows_here * window, first_block, integrals.shape[3])
    partial_value = contract(integral_rows, lax.all_gather(exchanged, "narrow", axis=2, tiled=True))
    ladder = lax.psum_scatter(
        partial_value.reshape(rows_here, window, all_pairs), "wide", scatter_dimension=2, tiled=True
    )
    swapped = lax.all_to_all(ladder, "narrow", split_axis=1, concat_axis=0, tiled=True)
    combined = ladder + jnp.transpose(swapped, (1, 0, 2))
    row_start = lax.axis_index("narrow") * rows_here
    own_virtuals = lax.dynamic_slice_in_dim(window_virtuals, row_start, rows_here, 0)
    row_energy = lookup(virt_energy, own_virtuals)
    column_energy = lookup(virt_energy, window_virtuals)
    pair_energy = lookup(occ_energy, pair_index[:, 0]) + lookup(occ_energy, pair_index[:, 1])
    denominator = (
        pair_energy[None, None, :] - row_energy[:, None, None] - column_energy[None, :, None]
    )
    return combined / denominator


def solution(mesh):
    in_specs = (
        P("wide", None, "narrow"),
        P("narrow", None, "wide", None),
        P("wide", None),
        P(),
        P(),
        P(),
    )
    out_specs = P("narrow", None, "wide")
    return jax.shard_map(shards, mesh=mesh, in_specs=in_specs, out_specs=out_specs, check_vma=False)
```

profile of v0, /device:TPU:0, one launch (start us, length us, event | category | flops | bytes accessed | tf_op | source)
XLA Modules:
  0.0 489.2 jit_solution(3291001078130395045)
XLA Ops:
  6.5 0.0 all-gather.2.cloned.1.call-start
  6.5 7.1 %copy.42 = f32[3,1024,512]{2,0,1:T(4,128)S(1)} copy(f32[3,1024,512]{2,1,0:T(8,128)} %param.6) | data formatting | bytes 12582912 | tf_op args[0]
  13.6 189.3 %all_to_all.36 = f32[3,1024,512]{2,0,1:T(4,128)S(1)} all-to-all(f32[3,1024,512]{2,0,1:T(4,128)S(1)} %copy.42), channel_id=1, replica_groups=mesh['wide'=16,'narrow'=2] {'wide'}, dimensions={1} | all-to-all | bytes 12582912 | tf_op jit(solution)/shard_map/all_to_all | solution.py:25
  202.9 2.0 copy.43
  205.0 1.2 copy.44
  206.2 0.0 copy-start.3
  206.2 0.0 copy-start.2
  206.2 0.0 copy-start.1
  206.2 0.0 copy-start
  206.3 6.3 %copy.45 = f32[48,64,512]{2,0,1:T(8,128)} copy(f32[48,64,512]{2,1,0:T(8,128)S(1)} %bitcast.30) | data formatting | bytes 12582912 | tf_op jit(solution)/shard_map/all_to_all | solution.py:25
  212.5 0.0 all-gather.2.cloned.1.call-update
  212.5 0.0 reduce-scatter.4.cloned.1.call-start
  212.6 0.1 dynamic_slice.3
  212.7 0.0 copy-done.2
  212.7 0.2 select_reduce_fusion.2
  212.9 0.2 select_reduce_fusion.1
  213.1 153.1 %all-gather.2.cloned.1.call-done = f32[48,64,1024]{2,0,1:T(8,128)} async-done(((f32[48,64,512]{2,0,1:T(8,128)}), f32[48,64,1024]{2,0,1:T(8,128)}) %all-gather.2.cloned.1.call-update) | async-done | bytes 12582928 | tf_op jit(solution)/shard_map/all_gather | solution.py:31
  366.2 50.3 %fusion.3 = f32[8,16,48]{2,1,0:T(8,128)S(1)} fusion(f32[48,64,1024]{2,0,1:T(8,128)} %all-gather.2.cloned.1.call-done, f32[8,16,64,1024]{3,2,1,0:T(8,128)} %param.7), kind=kOutput, calls=%fused_computation.3 | convolution fusion | flops 4831838208 | bytes 46161920 | tf_op jit(solution)/shard_map/dot_general | solution.py:15
  416.6 0.8 copy.47
  417.4 0.0 reduce-scatter.4.cloned.1.call-update
  417.4 0.1 broadcast_subtract_fusion
  417.5 53.7 %reduce-scatter.4.cloned.1.call-done = f32[8,16,3]{1,0,2:T(8,128)} async-done(((f32[8,16,48]{1,0,2:T(8,128)}), f32[8,16,3]{1,0,2:T(8,128)}) %reduce-scatter.4.cloned.1.call-update) | async-done | bytes 1552
  471.2 0.8 copy.48
  471.9 0.7 reshape.46
  472.6 3.2 all-to-all-start.1
  475.8 0.2 select_reduce_fusion
  476.0 3.6 all-to-all-done.1
  479.6 0.5 broadcast.40
  480.1 0.7 reduce
  480.8 0.1 reshape.47
  480.9 0.1 all_to_all.33
  481.0 1.4 fusion.8
  (6 shorter events, 0.0 us)
Async XLA Ops:
  6.5 359.7 %all-gather.2.cloned.1.call-start = ((), (), s32[]{:S(2)}) async-start(), calls=%async_computation.3 | async-start | bytes 18874368 | tf_op jit(solution)/shard_map/all_gather | solution.py:31
  206.2 6.4 %copy-start.3 = (s32[16]{0:T(128)S(1)}, s32[16]{0:T(128)}, u32[]{:S(2)}) copy-start(s32[16]{0:T(128)} %param.9) | copy-start | bytes 196
  206.2 6.5 %copy-start.2 = (s32[3,2]{0,1:T(2,128)S(1)}, s32[3,2]{0,1:T(2,128)}, u32[]{:S(2)}) copy-start(s32[3,2]{0,1:T(2,128)} %param.8) | copy-start | bytes 76
  206.2 6.5 %copy-start.1 = (f32[200]{0:T(256)S(1)}, f32[200]{0:T(256)}, u32[]{:S(2)}) copy-start(f32[200]{0:T(256)} %param.10) | copy-start | bytes 2404
  206.2 6.7 %copy-start = (f32[1024]{0:T(1024)S(1)}, f32[1024]{0:T(1024)}, u32[]{:S(2)}) copy-start(f32[1024]{0:T(1024)} %param.11) | copy-start | bytes 12292
  212.5 258.6 %reduce-scatter.4.cloned.1.call-start = ((), (), s32[]{:S(2)}) async-start(), calls=%async_computation.4 | async-start | bytes 208896
  472.6 7.0 %all-to-all-start.1 = ((f32[2,1,192]{2,1,0:T(1,128)}), f32[2,1,192]{2,1,0:T(1,128)S(1)}, u32[]{:S(2)}, u32[]{:S(2)}) async-start(f32[2,1,192]{2,1,0:T(1,128)} %reshape.46), calls=%async_computation.1 | async-start | bytes 4096 | tf_op jit(solution)/shard_map/all_to_all | solution.py:35
Sparse Core Ops, SparseCore 0:
  212.7 153.5 all-gather.1
  417.5 53.5 reduce-scatter.3
where the time goes:
time: 490 us; the launch traced here: 489 us
  waiting for transfers between devices  210 us (43%)
  blocking collectives  189 us (39%)
  matrix products  50.3 us (10%)
  local copies, waits for them, and re-layouts  19.7 us (4%)
  between operations  13.5 us (3%)
    all_to_all x1, blocking collectives, shards(): lax.all_to_all(amplitudes, 'wide', split_axis=1, concat_axis=0, tiled=True)  189 us
    all_gather x1, waiting for transfers between devices, shards(): lax.all_gather(exchanged, 'narrow', axis=2, tiled=True)  153 us
    unnamed x3, waiting for transfers between devices  53.7 us
    dot_general x1, matrix products, contract(): lax.dot_general(left_rows.reshape(left_rows.shape[0], -1), right_rows.res...  50.3 us
  transfers between devices with their start and end apart: 3, of which 3 were waited for; matrix products, arithmetic and copies ran while one was open for 0% of the time, Pallas kernels for 0%

commit v1 on v0

v1 whole, which is shorter than its diff:
```python
import functools

import jax
import jax.numpy as jnp
from jax import lax
from jax.experimental import pallas as pl
from jax.experimental.pallas import tpu as pltpu
from jax.sharding import PartitionSpec as P

INNER = 4
LANES = 128
GROUP = 8


def lookup(table, indices):
    matches = (indices[..., None] == jnp.arange(table.shape[0], dtype=jnp.int32)).astype(
        jnp.float32
    )
    return jnp.sum(matches * table, axis=-1)


def swap(value, axis, mask):
    size = lax.axis_size(axis)
    return lax.ppermute(value, axis, [(i, i ^ mask) for i in range(size)])


def pick(value, index, axis):
    return lax.dynamic_index_in_dim(value, index, axis, keepdims=False)


def halves(value):
    high = value.astype(jnp.bfloat16)
    low = (value - high.astype(jnp.float32)).astype(jnp.bfloat16)
    return jnp.concatenate([high, low], axis=0)


def contract_kernel(masks, near_count, narrow, partials, last, place_ref, *refs):
    refs = list(refs)
    out_ref, total, rows = refs[-3:]
    depth = refs[-4 - partials].shape[2]
    tiles = depth // LANES
    left_refs = refs[: narrow * tiles]
    near_refs = refs[narrow * tiles : narrow * tiles + near_count]
    far_refs = refs[narrow * tiles + near_count : narrow * tiles + near_count + narrow]
    partial_refs = refs[narrow * tiles + near_count + narrow : -3]
    step = pl.program_id(0)
    left_rows = left_refs[0].shape[0]
    height = rows.shape[0] // (narrow * tiles)
    pairs = height // GROUP

    @pl.when(step == 0)
    def _():
        total[...] = jnp.zeros_like(total)

    for j in range(narrow):
        for q in range(tiles):
            at = (j * tiles + q) * height
            lanes = pl.ds(q * LANES, LANES)
            for ref in near_refs:
                for core in range(ref.shape[0]):
                    count = ref.shape[2] * GROUP
                    rows[at : at + count, :] = ref[core, j, :, :, lanes].reshape(count, LANES)
                    at += count
            count = far_refs[j].shape[0] * GROUP
            rows[at : at + count, :] = far_refs[j][:, :, lanes].reshape(count, LANES)
    left_flat = [ref.reshape(left_rows * GROUP, LANES) for ref in left_refs]
    added = None
    for c in range(GROUP):
        left = [ref[pl.ds(c, left_rows, stride=GROUP), :] for ref in left_flat]
        right = [
            rows[pl.ds(n * height + c, pairs, stride=GROUP), :] for n in range(narrow * tiles)
        ]
        term = lax.dot_general(
            halves(jnp.concatenate(left, axis=1)),
            halves(jnp.concatenate(right, axis=1)),
            (((1,), (1,)), ((), ())),
            preferred_element_type=jnp.float32,
        )
        added = term if added is None else added + term
    total[...] += added

    @pl.when(step == pl.num_programs(0) - 1)
    def _():
        both = total[...]
        both = both[:left_rows] + both[left_rows:]
        turned = both.T
        value = turned[:pairs] + turned[pairs:]
        for ref in partial_refs:
            value = value + ref[...]
        if not last:
            out_ref[...] = value
        else:
            each = pairs // len(masks)
            for slot, mask in enumerate(masks):
                out_ref[place_ref[0] ^ mask] = value[slot * each : (slot + 1) * each]


def contract(place, integrals, near, far, partials, masks, start, last):
    left_rows, _, depth_all = integrals.shape
    narrow = len(far)
    depth = depth_all // narrow
    tiles = depth // LANES
    pairs = near[0].shape[0] * near[0].shape[2] * len(near) + far[0].shape[0]
    steps = far[0].shape[1] // GROUP
    first = start // GROUP

    def left_index(j, q, i, place):
        return (0, first + i, (place[1] ^ j) * tiles + q)

    in_specs = []
    for j in range(narrow):
        for q in range(tiles):
            in_specs.append(
                pl.BlockSpec((left_rows, GROUP, LANES), functools.partial(left_index, j, q))
            )
    for value in near:
        in_specs.append(
            pl.BlockSpec(value.shape[:3] + (GROUP, depth), lambda i, place: (0, 0, 0, first + i, 0))
        )
    for value in far:
        in_specs.append(pl.BlockSpec((value.shape[0], GROUP, depth), lambda i, place: (0, i, 0)))
    for value in partials:
        in_specs.append(pl.BlockSpec(value.shape, lambda i, place: (0, 0)))
    if last:
        shape = (len(masks), pairs // len(masks), left_rows)
        out_spec = pl.BlockSpec(shape, lambda i, place: (0, 0, 0))
    else:
        shape = (pairs, left_rows)
        out_spec = pl.BlockSpec(shape, lambda i, place: (0, 0))
    return pl.pallas_call(
        functools.partial(contract_kernel, masks, len(near), narrow, len(partials), last),
        out_shape=jax.ShapeDtypeStruct(shape, jnp.float32),
        grid_spec=pltpu.PrefetchScalarGridSpec(
            num_scalar_prefetch=1,
            grid=(steps,),
            in_specs=in_specs,
            out_specs=out_spec,
            scratch_shapes=[
                pltpu.VMEM((2 * left_rows, 2 * pairs), jnp.float32),
                pltpu.VMEM((pairs * GROUP * depth_all // LANES, LANES), jnp.float32),
            ],
        ),
        compiler_params=pltpu.CompilerParams(
            dimension_semantics=("arbitrary",), vmem_limit_bytes=32 << 20
        ),
        cost_estimate=pl.CostEstimate(
            flops=8 * left_rows * pairs * steps * GROUP * depth_all,
            bytes_accessed=4 * (left_rows + pairs) * steps * GROUP * depth_all,
            transcendentals=0,
        ),
    )(place, *([integrals] * (narrow * tiles)), *near, *far, *partials)


def inner_exchange(value, x_axis, place):
    core = place & 1
    high = (place >> 1) & 1
    kept = pick(value, core, x_axis + 1)
    come = swap(pick(value, 1 - core, x_axis + 1), "wide", 1)
    stay = jnp.stack([pick(kept, high, x_axis), pick(come, high, x_axis)])
    leave = jnp.stack([pick(kept, 1 - high, x_axis), pick(come, 1 - high, x_axis)])
    return stay, swap(leave, "wide", 2)


def row_chunks(rows):
    groups = rows // GROUP
    if groups < 4:
        return [GROUP] * groups
    last = max(1, groups // 8)
    middle = max(1, groups // 4)
    sizes = [groups - 2 * middle - last, middle, middle, last]
    return [size * GROUP for size in sizes]


def shards(amplitudes, integrals, pair_index, window_virtuals, occ_energy, virt_energy):
    wide = lax.axis_size("wide")
    narrow = lax.axis_size("narrow")
    outer = wide // INNER
    place = lax.axis_index("wide")
    side = lax.axis_index("narrow")
    outer_place = place // INNER
    pairs_here, _, depth = amplitudes.shape
    rows_here, window, rows, depth_all = integrals.shape
    near_masks = list(range(outer // 2))
    far_masks = list(range(outer // 2, outer))
    chunk_rows = row_chunks(rows)
    blocks = amplitudes.reshape(pairs_here, outer, 2, 2, rows, depth)

    first = chunk_rows[0]
    first_far = [
        swap(pick(blocks[..., :first, :], outer_place ^ k, 1), "wide", INNER * k)
        for k in far_masks
    ]
    near_own = []
    for k in near_masks:
        piece = pick(blocks, outer_place ^ k, 1)
        near_own.append(swap(piece, "wide", INNER * k) if k else piece)
    near_all = [
        jnp.stack([piece] + [swap(piece, "narrow", j) for j in range(1, narrow)])
        for piece in near_own
    ]
    near = []
    for piece in near_all:
        near.extend(inner_exchange(piece, 2, place))

    other = jnp.stack([pick(blocks[..., first:, :], outer_place ^ k, 1) for k in far_masks])
    other = jnp.stack(inner_exchange(other, 2, place))

    far_slots = INNER * len(far_masks) * pairs_here
    masks = [INNER * k + i for k in near_masks for i in range(INNER)]
    masks += [INNER * k + i for i in range(INNER) for k in far_masks]

    flat_integrals = integrals.reshape(rows_here * window, rows, depth_all)
    places = jnp.stack([place, side]).astype(jnp.int32)
    partials = []
    start = 0
    for number, count in enumerate(chunk_rows):
        if number == 0:
            own = jnp.stack(inner_exchange(jnp.stack(first_far), 2, place))
        else:
            begin = start - first
            own = jnp.stack(
                [
                    swap(other[:, :, n, :, begin : begin + count, :], "wide", INNER * k)
                    for n, k in enumerate(far_masks)
                ],
                axis=2,
            )
        own = own.reshape(far_slots, count, depth)
        far = [own] + [swap(own, "narrow", j) for j in range(1, narrow)]
        last = number == len(chunk_rows) - 1
        value = contract(
            places, flat_integrals, near, far, partials if last else [], masks, start, last
        )
        partials.append(value)
        start += count

    sent = jnp.broadcast_to(value[:, None], (wide, narrow) + value.shape[1:])
    sent = sent.reshape((wide * narrow,) + value.shape[1:])
    got = lax.all_to_all(sent, ("wide", "narrow"), 0, 0, tiled=True)
    got = got.reshape(wide, narrow, pairs_here, rows_here, window)
    whole = jnp.sum(got, axis=0).transpose(0, 2, 3, 1).reshape(window, window, pairs_here)
    row_start = side * rows_here
    combined = whole + jnp.transpose(whole, (1, 0, 2))
    combined = lax.dynamic_slice_in_dim(combined, row_start, rows_here, 0)
    own_virtuals = lax.dynamic_slice_in_dim(window_virtuals, row_start, rows_here, 0)
    row_energy = lookup(virt_energy, own_virtuals)
    column_energy = lookup(virt_energy, window_virtuals)
    pair_energy = lookup(occ_energy, pair_index[:, 0]) + lookup(occ_energy, pair_index[:, 1])
    denominator = (
        pair_energy[None, None, :] - row_energy[:, None, None] - column_energy[None, :, None]
    )
    return combined / denominator


def solution(mesh):
    in_specs = (
        P("wide", None, "narrow"),
        P("narrow", None, "wide", None),
        P("wide", None),
        P(),
        P(),
        P(),
    )
    out_specs = P("narrow", None, "wide")
    return jax.shard_map(shards, mesh=mesh, in_specs=in_specs, out_specs=out_specs, check_vma=False)
```

time: 490 us -> 276 us (0.56)
  blocking collectives: 189 us -> 0 us
  waiting for transfers between devices: 210 us -> 130 us
  starting transfers between devices: 3.26 us -> 75.8 us
  matrix products: 50.3 us -> 0 us
  Pallas kernels: 0 us -> 29.5 us
  other arithmetic: 2.72 us -> 21.4 us
  between operations: 13.5 us -> 0.4 us
    all_to_all x1 -> x0, blocking collectives: 189 us -> none  [shards(): lax.all_to_all(amplitudes, 'wide', split_axis=1, concat_axis=0, tiled=True)]
    all_gather x1 -> x0, waiting for transfers between devices: 153 us -> none  [shards(): lax.all_gather(exchanged, 'narrow', axis=2, tiled=True)]
    ppermute x0 -> x23, waiting for transfers between devices: none -> 123 us  [swap(): return lax.ppermute(value, axis, [(i, i ^ mask) for i in range(size)])]
    ppermute x0 -> x23, starting transfers between devices: none -> 72.5 us  [swap(): return lax.ppermute(value, axis, [(i, i ^ mask) for i in range(size)])]
    unnamed x3 -> x0, waiting for transfers between devices: 53.7 us -> none
    dot_general x1 -> x0, matrix products: 50.3 us -> none  [contract(): lax.dot_general(left_rows.reshape(left_rows.shape[0], -1), right_rows.res...]
    pallas_call x0 -> x4, Pallas kernels: none -> 29.5 us  [contract(): pl.pallas_call(functools.partial(contract_kernel, masks, len(near), narro...]
    another operation x0 -> x16, other arithmetic: none -> 12.5 us  [the longest x5 5.77 us: inner_exchange(): jnp.stack([pick(kept, 1 - high, x_axis), pick(come, 1 - high, x_axis)])]
  transfers between devices with their start and end apart: 3 -> 24, of which waited for: 3 -> 11; matrix products, arithmetic and copies ran while one was open for 0% -> 12% of each run, Pallas kernels for 0% -> 9%
where the time goes in v1:
time: 276 us
  waiting for transfers between devices  130 us (47%)
  starting transfers between devices  75.8 us (27%)
  Pallas kernels  29.5 us (11%)
  other arithmetic  21.4 us (8%)
  local copies, waits for them, and re-layouts  18.5 us (7%)
    ppermute x23, waiting for transfers between devices, swap(): return lax.ppermute(value, axis, [(i, i ^ mask) for i in range(size)])  123 us
    ppermute x23, starting transfers between devices, swap(): return lax.ppermute(value, axis, [(i, i ^ mask) for i in range(size)])  72.5 us
    pallas_call x4, Pallas kernels, contract(): pl.pallas_call(functools.partial(contract_kernel, masks, len(near), narro...  29.5 us
    all_to_all x1, waiting for transfers between devices, shards(): got = lax.all_to_all(sent, ('wide', 'narrow'), 0, 0, tiled=True)  7.4 us
    another operation x5, other arithmetic, inner_exchange(): jnp.stack([pick(kept, 1 - high, x_axis), pick(come, 1 - high, x_axis)])  5.77 us
  transfers between devices with their start and end apart: 24, of which 11 were waited for; matrix products, arithmetic and copies ran while one was open for 12% of the time, Pallas kernels for 9%

profile of v1, /device:TPU:0, one launch (start us, length us, event | category | flops | bytes accessed | tf_op | source)
XLA Modules:
  0.0 275.6 jit_solution(12883403507074688973)
XLA Ops:
  0.0 3.6 %dynamic-slice_bitcast_fusion = (f32[3,2,2,64,512]{4,3,2,1,0:T(8,128)S(1)}, f32[3,2,2,64,512]{4,3,2,1,0:T(8,128)}, f32[1,3,2,2,64,512]{5,4,3,2,1,0:T(8,128)S(1)}) fusion(f32[3,4,2,2,64,512]{5,4,3,2,1,0:T(8,128)} %bitcast.146, s32[]{:T(128)S(6)} %select_n.79, s32[]{:T(128)S(6)} %select_n.71), kind=kLoop, calls=%fused_computation.32 | loop fusion | bytes 7864328 | tf_op jit(solution)/shard_map/jit(dynamic_index_in_dim)/squeeze | solution.py:28
  3.6 3.0 %collective-permute-start.3 = (f32[3,2,2,64,512]{4,3,2,1,0:T(8,128)S(1)}, f32[3,2,2,64,512]{4,3,2,1,0:T(8,128)}, u32[]{:S(2)}, u32[]{:S(2)}) collective-permute-start(f32[3,2,2,64,512]{4,3,2,1,0:T(8,128)S(1)} %get-tuple-element.7), channel_id=1, source_target_pairs={{0,8},{2,10},{4,12},{6,14},{8,0},{10,2},{12,4},{14,6},{16,24},{18,... | collective-permute-start | bytes 4718600 | tf_op jit(solution)/shard_map/ppermute | solution.py:24
  6.6 1.5 collective-permute-start
  8.1 33.0 %collective-permute-done.3 = f32[3,2,2,64,512]{4,3,2,1,0:T(8,128)} collective-permute-done((f32[3,2,2,64,512]{4,3,2,1,0:T(8,128)S(1)}, f32[3,2,2,64,512]{4,3,2,1,0:T(8,128)}, u32[]{:S(2)}, u32[]{:S(2)}) %collective-permute-start.3) | collective-permute-done | bytes 1572896 | tf_op jit(solution)/shard_map/ppermute | solution.py:24
  41.1 1.7 collective-permute-start.4
  42.8 4.8 %slice.42 = f32[3,4,2,2,40,512]{5,4,3,2,1,0:T(8,128)} slice(f32[3,4,2,2,64,512]{5,4,3,2,1,0:T(8,128)} %bitcast.147), slice={[0:3], [0:4], [0:2], [0:2], [24:64], [0:512]} | slice | bytes 7864320 | tf_op jit(solution)/shard_map/slice | solution.py:205
  47.6 1.7 dynamic-slice_bitcast_fusion.3
  50.4 1.9 slice.43
  53.4 2.6 collective-permute-start.12
  60.0 16.9 %collective-permute-done.4 = f32[3,2,2,64,512]{4,3,2,1,0:T(8,128)} collective-permute-done((f32[3,2,2,64,512]{4,3,2,1,0:T(8,128)}, f32[3,2,2,64,512]{4,3,2,1,0:T(8,128)}, u32[]{:S(2)}, u32[]{:S(2)}) %collective-permute-start.4) | collective-permute-done | bytes 1572896 | tf_op jit(solution)/shard_map/ppermute | solution.py:24
  77.0 1.5 fusion.1
  80.0 16.0 %collective-permute-done.12 = f32[3,2,2,24,512]{4,3,2,1,0:T(8,128)} collective-permute-done((f32[3,2,2,24,512]{4,3,2,1,0:T(8,128)}, f32[3,2,2,24,512]{4,3,2,1,0:T(8,128)}, u32[]{:S(2)}, u32[]{:S(2)}) %collective-permute-start.12) | collective-permute-done | bytes 589856 | tf_op jit(solution)/shard_map/ppermute | solution.py:24
  100.0 1.6 collective-permute-start.15
  103.7 3.7 %collective-permute-start.10 = (f32[2,2,3,8,512]{4,3,2,1,0:T(8,128)}, f32[2,2,3,8,512]{4,3,2,1,0:T(8,128)}, u32[]{:S(2)}, u32[]{:S(2)}) collective-permute-start(f32[2,2,3,8,512]{4,3,2,1,0:T(8,128)} %get-tuple-element.23), channel_id=1, source_target_pairs={{0,24},{2,26},{4,28},{6,30},{8,16},{10,18},{12,20},{14,22},{16,8},... | collective-permute-start | bytes 589832 | tf_op jit(solution)/shard_map/ppermute | solution.py:24
  108.7 3.1 %fusion.7 = (f32[1,2,3,64,512]{4,3,2,1,0:T(8,128)S(1)}, f32[1,2,3,64,512]{4,3,2,1,0:T(8,128)}, f32[1,2,3,64,512]{4,3,2,1,0:T(8,128)}, f32[1,2,3,64,512]{4,3,2,1,0:T(8,128)S(1)}) fusion(s32[]{:T(128)S(6)} %select_n.78, s32[]{:T(128)S(6)} %select_n.75, f32[1,3,2,2,64,512]{5,4,3,2,1,0:T(8,128)} %bitcast.13, f32[1,3,2,2,64,512]{5,4,3,2,1,0:T(8,128)} %bitcast.14, ...), kind=kLoop, calls=%fused_computation.43 | loop fusion | flops 786432 | bytes 9437196 | tf_op jit(solution)/shard_map/stack | solution.py:160
  111.8 24.4 %collective-permute-start.17 = (f32[2,2,3,16,512]{4,3,2,1,0:T(8,128)}, f32[2,2,3,16,512]{4,3,2,1,0:T(8,128)}, u32[]{:S(2)}, u32[]{:S(2)}) collective-permute-start(f32[2,2,3,16,512]{4,3,2,1,0:T(8,128)} %get-tuple-element.20), channel_id=1, source_target_pairs={{0,16},{2,18},{4,20},{6,22},{8,24},{10,26},{12,28},{14,30},{16,0},... | collective-permute-start | bytes 1179656 | tf_op jit(solution)/shard_map/ppermute | solution.py:24
  136.2 1.5 dynamic-slice_bitcast_fusion.5
  141.6 1.5 collective-permute-start.6
  144.4 18.9 %collective-permute-start.20 = (f32[2,2,3,16,512]{4,3,2,1,0:T(8,128)}, f32[2,2,3,16,512]{4,3,2,1,0:T(8,128)S(1)}, u32[]{:S(2)}, u32[]{:S(2)}) collective-permute-start(f32[2,2,3,16,512]{4,3,2,1,0:T(8,128)} %get-tuple-element.18), channel_id=1, source_target_pairs={{0,16},{2,18},{4,20},{6,22},{8,24},{10,26},{12,28},{14,30},{16,0},... | collective-permute-start | bytes 1179656 | tf_op jit(solution)/shard_map/ppermute | solution.py:24
  165.3 12.7 %collective-permute-done.17 = f32[2,2,3,16,512]{4,3,2,1,0:T(8,128)} collective-permute-done((f32[2,2,3,16,512]{4,3,2,1,0:T(8,128)}, f32[2,2,3,16,512]{4,3,2,1,0:T(8,128)}, u32[]{:S(2)}, u32[]{:S(2)}) %collective-permute-start.17) | collective-permute-done | bytes 393248 | tf_op jit(solution)/shard_map/ppermute | solution.py:24
  179.3 9.1 %collective-permute-start.9 = (f32[2,2,3,8,512]{4,3,2,1,0:T(8,128)S(1)}, f32[2,2,3,8,512]{4,3,2,1,0:T(8,128)S(1)}, u32[]{:S(2)}, u32[]{:S(2)}) collective-permute-start(f32[2,2,3,8,512]{4,3,2,1,0:T(8,128)S(1)} %copy-done.6), channel_id=1, source_target_pairs={{0,16},{2,18},{4,20},{6,22},{8,24},{10,26},{12,28},{14,30},{16,0},... | collective-permute-start | bytes 589832 | tf_op jit(solution)/shard_map/ppermute | solution.py:24
  188.4 10.6 %collective-permute-done.20 = f32[2,2,3,16,512]{4,3,2,1,0:T(8,128)S(1)} collective-permute-done((f32[2,2,3,16,512]{4,3,2,1,0:T(8,128)}, f32[2,2,3,16,512]{4,3,2,1,0:T(8,128)S(1)}, u32[]{:S(2)}, u32[]{:S(2)}) %collective-permute-start.20) | collective-permute-done | bytes 393248 | tf_op jit(solution)/shard_map/ppermute | solution.py:24
  199.3 3.1 %collective-permute-done.9 = f32[2,2,3,8,512]{4,3,2,1,0:T(8,128)S(1)} collective-permute-done((f32[2,2,3,8,512]{4,3,2,1,0:T(8,128)S(1)}, f32[2,2,3,8,512]{4,3,2,1,0:T(8,128)S(1)}, u32[]{:S(2)}, u32[]{:S(2)}) %collective-permute-start.9) | collective-permute-done | bytes 196640 | tf_op jit(solution)/shard_map/ppermute | solution.py:24
  203.1 1.7 pad_maximum_fusion.10
  205.0 19.0 %collective-permute-done.19.refs_13_ = f32[24,16,512]{2,1,0:T(8,128)S(1)} collective-permute-done((f32[24,16,512]{2,1,0:T(8,128)S(1)}, f32[24,16,512]{2,1,0:T(8,128)S(1)}, u32[]{:S(2)}, u32[]{:S(2)}) %collective-permute-start.19) | collective-permute-done | bytes 786464 | tf_op jit(solution)/shard_map/ppermute | solution.py:24
  224.2 7.4 %shard_map.65.refs_15_ = f32[48,128]{1,0:T(8,128)S(1)} custom-call(s32[2]{0:T(128)S(1)} %pad_add_fusion.place_ref, f32[128,64,1024]{2,1,0:T(8,128)} %bitcast.114, f32[128,64,1024]{2,1,0:T(8,128)} %bitcast.115, f32[128,64,1024]{2,1,0:T(8,128)} %bitcast.116, f32[128,64,1024]{2,1,0:T(8,128)} %bitcast.117, f32[128,64,1024]{2,1,0:T(8,128)} %bitcast.118, ...), custom_call_target="tpu_custom_call" | custom-call | flops 805306368 | bytes 11534336 | tf_op jit(solution)/shard_map/pallas_call | solution.py:130
  231.5 9.3 %collective-permute-done.22.refs_13_ = f32[24,16,512]{2,1,0:T(8,128)S(1)} collective-permute-done((f32[24,16,512]{2,1,0:T(8,128)S(1)}, f32[24,16,512]{2,1,0:T(8,128)S(1)}, u32[]{:S(2)}, u32[]{:S(2)}) %collective-permute-start.22) | collective-permute-done | bytes 786464 | tf_op jit(solution)/shard_map/ppermute | solution.py:24
  240.8 7.2 %shard_map.66.refs_16_ = f32[48,128]{1,0:T(8,128)S(1)} custom-call(s32[2]{0:T(128)S(1)} %pad_add_fusion.place_ref, f32[128,64,1024]{2,1,0:T(8,128)} %bitcast.129, f32[128,64,1024]{2,1,0:T(8,128)} %bitcast.123, f32[128,64,1024]{2,1,0:T(8,128)} %bitcast.124, f32[128,64,1024]{2,1,0:T(8,128)} %bitcast.125, f32[128,64,1024]{2,1,0:T(8,128)} %bitcast.126, ...), custom_call_target="tpu_custom_call" | custom-call | flops 805306368 | bytes 11534336 | tf_op jit(solution)/shard_map/pallas_call | solution.py:130
  248.0 9.9 %shard_map.64.refs_14_ = f32[48,128]{1,0:T(8,128)S(1)} custom-call(s32[2]{0:T(128)S(1)} %pad_add_fusion.place_ref, f32[128,64,1024]{2,1,0:T(8,128)} %bitcast.130, f32[128,64,1024]{2,1,0:T(8,128)} %bitcast.131, f32[128,64,1024]{2,1,0:T(8,128)} %bitcast.132, f32[128,64,1024]{2,1,0:T(8,128)} %bitcast.133, f32[128,64,1024]{2,1,0:T(8,128)} %bitcast.134, ...), custom_call_target="tpu_custom_call" | custom-call | flops 1207959552 | bytes 17301504 | tf_op jit(solution)/shard_map/pallas_call | solution.py:130
  258.0 5.1 %shard_map.67 = f32[16,3,128]{2,1,0:T(4,128)S(1)} custom-call(s32[2]{0:T(128)S(1)} %pad_add_fusion.place_ref, f32[128,64,1024]{2,1,0:T(8,128)} %bitcast.138, f32[128,64,1024]{2,1,0:T(8,128)} %bitcast.139, f32[128,64,1024]{2,1,0:T(8,128)} %bitcast.140, f32[128,64,1024]{2,1,0:T(8,128)} %bitcast.141, f32[128,64,1024]{2,1,0:T(8,128)} %bitcast.142, ...), custom_call_target="tpu_custom_call" | custom-call | flops 402653184 | bytes 5767168 | tf_op jit(solution)/shard_map/pallas_call | solution.py:130
  263.7 3.3 %all-to-all-start = ((f32[32,3,128]{2,1,0:T(4,128)}), f32[32,3,128]{2,1,0:T(4,128)S(1)}, u32[]{:S(2)}, u32[]{:S(2)}) async-start(f32[32,3,128]{2,1,0:T(4,128)} %bitcast.57), calls=%async_computation | async-start | bytes 131072 | tf_op jit(solution)/shard_map/all_to_all | solution.py:239
  267.3 7.4 %all-to-all-done = f32[32,3,128]{2,1,0:T(4,128)S(1)} async-done(((f32[32,3,128]{2,1,0:T(4,128)}), f32[32,3,128]{2,1,0:T(4,128)S(1)}, u32[]{:S(2)}, u32[]{:S(2)}) %all-to-all-start) | async-done | bytes 49184 | tf_op jit(solution)/shard_map/all_to_all | solution.py:239
  (93 shorter events, 26.8 us)
Async XLA Ops:
  3.6 37.5 %collective-permute-start.3 = (f32[3,2,2,64,512]{4,3,2,1,0:T(8,128)S(1)}, f32[3,2,2,64,512]{4,3,2,1,0:T(8,128)}, u32[]{:S(2)}, u32[]{:S(2)}) collective-permute-start(f32[3,2,2,64,512]{4,3,2,1,0:T(8,128)S(1)} %get-tuple-element.7), channel_id=1, source_target_pairs={{0,8},{2,10},{4,12},{6,14},{8,0},{10,2},{12,4},{14,6},{16,24},{18,... | collective-permute-start | bytes 4718600 | tf_op jit(solution)/shard_map/ppermute | solution.py:24
  6.6 52.1 %collective-permute-start = (f32[3,2,2,64,512]{4,3,2,1,0:T(8,128)}, f32[3,2,2,64,512]{4,3,2,1,0:T(8,128)}, u32[]{:S(2)}, u32[]{:S(2)}) collective-permute-start(f32[3,2,2,64,512]{4,3,2,1,0:T(8,128)} %get-tuple-element.8), channel_id=1, source_target_pairs={{0,1},{1,0},{2,3},{3,2},{4,5},{5,4},{6,7},{7,6},{8,9},{9,8},{10,11... | collective-permute-start | bytes 4718600 | tf_op jit(solution)/shard_map/ppermute | solution.py:24
  41.1 35.9 %collective-permute-start.4 = (f32[3,2,2,64,512]{4,3,2,1,0:T(8,128)}, f32[3,2,2,64,512]{4,3,2,1,0:T(8,128)}, u32[]{:S(2)}, u32[]{:S(2)}) collective-permute-start(f32[3,2,2,64,512]{4,3,2,1,0:T(8,128)} %collective-permute-done.3), channel_id=1, source_target_pairs={{0,1},{1,0},{2,3},{3,2},{4,5},{5,4},{6,7},{7,6},{8,9},{9,8},{10,11... | collective-permute-start | bytes 4718600 | tf_op jit(solution)/shard_map/ppermute | solution.py:24
  50.4 7.1 %collective-permute-start.7 = (f32[2,3,2,40,512]{4,3,2,1,0:T(8,128)}, f32[2,3,2,40,512]{4,3,2,1,0:T(8,128)}, u32[]{:S(2)}, u32[]{:S(2)}) collective-permute-start(f32[2,3,2,40,512]{4,3,2,1,0:T(8,128)} %fusion.5), channel_id=1, source_target_pairs={{0,2},{2,0},{4,6},{6,4},{8,10},{10,8},{12,14},{14,12},{16,18},{18,... | collective-permute-start | bytes 2949128 | tf_op jit(solution)/shard_map/ppermute | solution.py:24
  53.4 42.6 %collective-permute-start.12 = (f32[3,2,2,24,512]{4,3,2,1,0:T(8,128)}, f32[3,2,2,24,512]{4,3,2,1,0:T(8,128)}, u32[]{:S(2)}, u32[]{:S(2)}) collective-permute-start(f32[3,2,2,24,512]{4,3,2,1,0:T(8,128)} %get-tuple-element.17), channel_id=1, source_target_pairs={{0,16},{2,18},{4,20},{6,22},{8,24},{10,26},{12,28},{14,30},{16,0},... | collective-permute-start | bytes 1769480 | tf_op jit(solution)/shard_map/ppermute | solution.py:24
  56.0 40.0 %collective-permute-start.13 = (f32[3,2,2,24,512]{4,3,2,1,0:T(8,128)}, f32[3,2,2,24,512]{4,3,2,1,0:T(8,128)}, u32[]{:S(2)}, u32[]{:S(2)}) collective-permute-start(f32[3,2,2,24,512]{4,3,2,1,0:T(8,128)} %get-tuple-element.16), channel_id=1, source_target_pairs={{0,24},{2,26},{4,28},{6,30},{8,16},{10,18},{12,20},{14,22},{16,8},... | collective-permute-start | bytes 1769480 | tf_op jit(solution)/shard_map/ppermute | solution.py:24
  60.0 51.8 %collective-permute-start.1 = (f32[2,3,2,64,512]{4,3,2,1,0:T(8,128)S(1)}, f32[2,3,2,64,512]{4,3,2,1,0:T(8,128)S(1)}, u32[]{:S(2)}, u32[]{:S(2)}) collective-permute-start(f32[2,3,2,64,512]{4,3,2,1,0:T(8,128)S(1)} %fusion.3), channel_id=1, source_target_pairs={{0,2},{2,0},{4,6},{6,4},{8,10},{10,8},{12,14},{14,12},{16,18},{18,... | collective-permute-start | bytes 4718600 | tf_op jit(solution)/shard_map/ppermute | solution.py:24
  78.5 57.7 %collective-permute-start.5 = (f32[2,3,2,64,512]{4,3,2,1,0:T(8,128)S(1)}, f32[2,3,2,64,512]{4,3,2,1,0:T(8,128)S(1)}, u32[]{:S(2)}, u32[]{:S(2)}) collective-permute-start(f32[2,3,2,64,512]{4,3,2,1,0:T(8,128)S(1)} %fusion.1), channel_id=1, source_target_pairs={{0,2},{2,0},{4,6},{6,4},{8,10},{10,8},{12,14},{14,12},{16,18},{18,... | collective-permute-start | bytes 4718600 | tf_op jit(solution)/shard_map/ppermute | solution.py:24
  78.6 24.2 %collective-permute-start.8 = (f32[2,2,3,40,512]{4,3,2,0,1:T(8,128)S(1)}, f32[2,2,3,40,512]{4,3,2,0,1:T(8,128)S(1)}, u32[]{:S(2)}, u32[]{:S(2)}) collective-permute-start(f32[2,2,3,40,512]{4,3,2,0,1:T(8,128)S(1)} %pad_maximum_fusion.5), channel_id=1, source_target_pairs={{0,4},{2,6},{4,0},{6,2},{8,12},{10,14},{12,8},{14,10},{16,20},{18,... | collective-permute-start | bytes 2949128 | tf_op jit(solution)/shard_map/ppermute | solution.py:24
  97.1 2.1 collective-permute-start.14
  100.0 40.8 %collective-permute-start.15 = (f32[2,2,3,24,512]{4,3,2,1,0:T(8,128)S(1)}, f32[2,2,3,24,512]{4,3,2,1,0:T(8,128)S(1)}, u32[]{:S(2)}, u32[]{:S(2)}) collective-permute-start(f32[2,2,3,24,512]{4,3,2,1,0:T(8,128)S(1)} %pad_maximum_fusion.8), channel_id=1, source_target_pairs={{0,4},{2,6},{4,0},{6,2},{8,12},{10,14},{12,8},{14,10},{16,20},{18,... | collective-permute-start | bytes 1769480 | tf_op jit(solution)/shard_map/ppermute | solution.py:24
  103.7 39.8 %collective-permute-start.10 = (f32[2,2,3,8,512]{4,3,2,1,0:T(8,128)}, f32[2,2,3,8,512]{4,3,2,1,0:T(8,128)}, u32[]{:S(2)}, u32[]{:S(2)}) collective-permute-start(f32[2,2,3,8,512]{4,3,2,1,0:T(8,128)} %get-tuple-element.23), channel_id=1, source_target_pairs={{0,24},{2,26},{4,28},{6,30},{8,16},{10,18},{12,20},{14,22},{16,8},... | collective-permute-start | bytes 589832 | tf_op jit(solution)/shard_map/ppermute | solution.py:24
  108.6 35.8 %collective-permute-start.18 = (f32[2,2,3,16,512]{4,3,2,1,0:T(8,128)}, f32[2,2,3,16,512]{4,3,2,1,0:T(8,128)}, u32[]{:S(2)}, u32[]{:S(2)}) collective-permute-start(f32[2,2,3,16,512]{4,3,2,1,0:T(8,128)} %get-tuple-element.19), channel_id=1, source_target_pairs={{0,24},{2,26},{4,28},{6,30},{8,16},{10,18},{12,20},{14,22},{16,8},... | collective-permute-start | bytes 1179656 | tf_op jit(solution)/shard_map/ppermute | solution.py:24
  111.8 66.2 %collective-permute-start.17 = (f32[2,2,3,16,512]{4,3,2,1,0:T(8,128)}, f32[2,2,3,16,512]{4,3,2,1,0:T(8,128)}, u32[]{:S(2)}, u32[]{:S(2)}) collective-permute-start(f32[2,2,3,16,512]{4,3,2,1,0:T(8,128)} %get-tuple-element.20), channel_id=1, source_target_pairs={{0,16},{2,18},{4,20},{6,22},{8,24},{10,26},{12,28},{14,30},{16,0},... | collective-permute-start | bytes 1179656 | tf_op jit(solution)/shard_map/ppermute | solution.py:24
  139.0 85.2 %collective-permute-start.2 = (f32[2,2,3,64,512]{4,3,2,1,0:T(8,128)}, f32[2,2,3,64,512]{4,3,2,1,0:T(8,128)S(1)}, u32[]{:S(2)}, u32[]{:S(2)}) collective-permute-start(f32[2,2,3,64,512]{4,3,2,1,0:T(8,128)} %pad_maximum_fusion.1), channel_id=1, source_target_pairs={{0,4},{2,6},{4,0},{6,2},{8,12},{10,14},{12,8},{14,10},{16,20},{18,... | collective-permute-start | bytes 4718600 | tf_op jit(solution)/shard_map/ppermute | solution.py:24
  141.6 82.6 %collective-permute-start.6 = (f32[2,2,3,64,512]{4,3,2,1,0:T(8,128)}, f32[2,2,3,64,512]{4,3,2,1,0:T(8,128)S(1)}, u32[]{:S(2)}, u32[]{:S(2)}) collective-permute-start(f32[2,2,3,64,512]{4,3,2,1,0:T(8,128)} %pad_maximum_fusion.3), channel_id=1, source_target_pairs={{0,4},{2,6},{4,0},{6,2},{8,12},{10,14},{12,8},{14,10},{16,20},{18,... | collective-permute-start | bytes 4718600 | tf_op jit(solution)/shard_map/ppermute | solution.py:24
  143.1 21.2 %copy-start.5 = (f32[2,2,3,24,512]{4,3,2,1,0:T(8,128)S(1)}, f32[2,2,3,24,512]{4,3,2,1,0:T(8,128)}, u32[]{:S(2)}) copy-start(f32[2,2,3,24,512]{4,3,2,1,0:T(8,128)} %copy-done.4) | copy-start | bytes 1769476
  143.4 35.9 %collective-permute-start.21 = (f32[2,2,3,16,512]{4,3,2,1,0:T(8,128)}, f32[2,2,3,16,512]{4,3,2,1,0:T(8,128)S(1)}, u32[]{:S(2)}, u32[]{:S(2)}) collective-permute-start(f32[2,2,3,16,512]{4,3,2,1,0:T(8,128)} %get-tuple-element.21), channel_id=1, source_target_pairs={{0,24},{2,26},{4,28},{6,30},{8,16},{10,18},{12,20},{14,22},{16,8},... | collective-permute-start | bytes 1179656 | tf_op jit(solution)/shard_map/ppermute | solution.py:24
  144.4 54.6 %collective-permute-start.20 = (f32[2,2,3,16,512]{4,3,2,1,0:T(8,128)}, f32[2,2,3,16,512]{4,3,2,1,0:T(8,128)S(1)}, u32[]{:S(2)}, u32[]{:S(2)}) collective-permute-start(f32[2,2,3,16,512]{4,3,2,1,0:T(8,128)} %get-tuple-element.18), channel_id=1, source_target_pairs={{0,16},{2,18},{4,20},{6,22},{8,24},{10,26},{12,28},{14,30},{16,0},... | collective-permute-start | bytes 1179656 | tf_op jit(solution)/shard_map/ppermute | solution.py:24
  178.0 70.0 %collective-permute-start.16 = (f32[24,24,512]{2,1,0:T(8,128)}, f32[24,24,512]{2,1,0:T(8,128)}, u32[]{:S(2)}, u32[]{:S(2)}) collective-permute-start(f32[24,24,512]{2,1,0:T(8,128)} %bitcast.46.refs_12_), channel_id=1, source_target_pairs={{0,1},{1,0},{2,3},{3,2},{4,5},{5,4},{6,7},{7,6},{8,9},{9,8},{10,11... | collective-permute-start | bytes 3538952 | tf_op jit(solution)/shard_map/ppermute | solution.py:24
  178.0 21.0 %copy-start.7 = (f32[1024]{0:T(1024)S(1)}, f32[1024]{0:T(1024)}, u32[]{:S(2)}) copy-start(f32[1024]{0:T(1024)} %param.11) | copy-start | bytes 12292
  179.3 23.1 %collective-permute-start.9 = (f32[2,2,3,8,512]{4,3,2,1,0:T(8,128)S(1)}, f32[2,2,3,8,512]{4,3,2,1,0:T(8,128)S(1)}, u32[]{:S(2)}, u32[]{:S(2)}) collective-permute-start(f32[2,2,3,8,512]{4,3,2,1,0:T(8,128)S(1)} %copy-done.6), channel_id=1, source_target_pairs={{0,16},{2,18},{4,20},{6,22},{8,24},{10,26},{12,28},{14,30},{16,0},... | collective-permute-start | bytes 589832 | tf_op jit(solution)/shard_map/ppermute | solution.py:24
  199.0 25.0 %collective-permute-start.19 = (f32[24,16,512]{2,1,0:T(8,128)S(1)}, f32[24,16,512]{2,1,0:T(8,128)S(1)}, u32[]{:S(2)}, u32[]{:S(2)}) collective-permute-start(f32[24,16,512]{2,1,0:T(8,128)S(1)} %bitcast.110), channel_id=1, source_target_pairs={{0,1},{1,0},{2,3},{3,2},{4,5},{5,4},{6,7},{7,6},{8,9},{9,8},{10,11... | collective-permute-start | bytes 2359304 | tf_op jit(solution)/shard_map/ppermute | solution.py:24
  199.2 5.6 %copy-start.1 = (f32[1,2,3,64,512]{4,3,2,1,0:T(8,128)S(1)}, f32[1,2,3,64,512]{4,3,2,1,0:T(8,128)}, u32[]{:S(2)}) copy-start(f32[1,2,3,64,512]{4,3,2,1,0:T(8,128)} %get-tuple-element.40) | copy-start | bytes 2359300
  202.4 38.4 %collective-permute-start.22 = (f32[24,16,512]{2,1,0:T(8,128)S(1)}, f32[24,16,512]{2,1,0:T(8,128)S(1)}, u32[]{:S(2)}, u32[]{:S(2)}) collective-permute-start(f32[24,16,512]{2,1,0:T(8,128)S(1)} %bitcast.112), channel_id=1, source_target_pairs={{0,1},{1,0},{2,3},{3,2},{4,5},{5,4},{6,7},{7,6},{8,9},{9,8},{10,11... | collective-permute-start | bytes 2359304 | tf_op jit(solution)/shard_map/ppermute | solution.py:24
  204.8 19.2 %copy-start = (f32[1,2,3,64,512]{4,3,2,1,0:T(8,128)S(1)}, f32[1,2,3,64,512]{4,3,2,1,0:T(8,128)}, u32[]{:S(2)}) copy-start(f32[1,2,3,64,512]{4,3,2,1,0:T(8,128)} %get-tuple-element.13) | copy-start | bytes 2359300
  204.8 19.2 %copy-start.2 = (f32[1,2,3,64,512]{4,3,2,1,0:T(8,128)S(1)}, f32[1,2,3,64,512]{4,3,2,1,0:T(8,128)}, u32[]{:S(2)}) copy-start(f32[1,2,3,64,512]{4,3,2,1,0:T(8,128)} %get-tuple-element.27) | copy-start | bytes 2359300
  224.0 34.0 %collective-permute-start.11 = (f32[24,8,512]{2,1,0:T(8,128)}, f32[24,8,512]{2,1,0:T(8,128)}, u32[]{:S(2)}, u32[]{:S(2)}) collective-permute-start(f32[24,8,512]{2,1,0:T(8,128)} %bitcast.34.refs_12_), channel_id=1, source_target_pairs={{0,1},{1,0},{2,3},{3,2},{4,5},{5,4},{6,7},{7,6},{8,9},{9,8},{10,11... | collective-permute-start | bytes 1179656 | tf_op jit(solution)/shard_map/ppermute | solution.py:24
  257.9 9.1 %copy-start.8 = (f32[1024]{0:T(1024)S(1)}, f32[1024]{0:T(1024)}, u32[]{:S(2)}) copy-start(f32[1024]{0:T(1024)} %param.11) | copy-start | bytes 12292
  257.9 9.1 %copy-start.13 = (s32[16]{0:T(128)S(1)}, s32[16]{0:T(128)}, u32[]{:S(2)}) copy-start(s32[16]{0:T(128)} %param.9) | copy-start | bytes 196
  257.9 17.0 %copy-start.9 = (f32[8,3]{0,1:T(4,128)S(1)}, f32[8,3]{0,1:T(4,128)}, u32[]{:S(2)}) copy-start(f32[8,3]{0,1:T(4,128)} %broadcast_subtract_fusion) | copy-start | bytes 292
  263.7 10.9 %all-to-all-start = ((f32[32,3,128]{2,1,0:T(4,128)}), f32[32,3,128]{2,1,0:T(4,128)S(1)}, u32[]{:S(2)}, u32[]{:S(2)}) async-start(f32[32,3,128]{2,1,0:T(4,128)} %bitcast.57), calls=%async_computation | async-start | bytes 131072 | tf_op jit(solution)/shard_map/all_to_all | solution.py:239
  (6 other events, 18.6 us)

commit v2 on v1

v2 whole, which is shorter than its diff:
```python
import functools

import jax
import jax.numpy as jnp
from jax import lax
from jax.experimental import pallas as pl
from jax.experimental.pallas import tpu as pltpu
from jax.sharding import PartitionSpec as P

INNER = 4
LANES = 128
EARLY = 4
GROUP = 8


def lookup(table, indices):
    matches = (indices[..., None] == jnp.arange(table.shape[0], dtype=jnp.int32)).astype(
        jnp.float32
    )
    return jnp.sum(matches * table, axis=-1)


def swap(value, axis, mask):
    size = lax.axis_size(axis)
    return lax.ppermute(value, axis, [(i, i ^ mask) for i in range(size)])


def halves(value):
    high = value.astype(jnp.bfloat16)
    low = (value - high.astype(jnp.float32)).astype(jnp.bfloat16)
    return jnp.concatenate([high, low], axis=0)


def contract_kernel(masks, near_count, far_count, narrow, partials, last, place_ref, *refs):
    refs = list(refs)
    out_ref, total, rows = refs[-3:]
    near_size = narrow + 2
    depth = refs[-4 - partials].shape[-1]
    tiles = depth // LANES
    near_at = narrow * tiles
    far_at = near_at + near_count * near_size
    left_refs = refs[:near_at]
    near_refs = [
        refs[near_at + n * near_size : near_at + (n + 1) * near_size] for n in range(near_count)
    ]
    far_refs = [refs[far_at + n * narrow : far_at + (n + 1) * narrow] for n in range(far_count)]
    partial_refs = refs[far_at + far_count * narrow : -3]
    step = pl.program_id(0)
    left_rows = left_refs[0].shape[0]
    height = rows.shape[0] // (narrow * tiles)
    pairs = height // GROUP

    @pl.when(step == 0)
    def _():
        total[...] = jnp.zeros_like(total)

    for j in range(narrow):
        for q in range(tiles):
            at = (j * tiles + q) * height
            lanes = pl.ds(q * LANES, LANES)
            for own_and_come in near_refs:
                come, inward = own_and_come[narrow:]
                count = come.shape[1] * GROUP
                for part in (
                    own_and_come[j][:, 0, 0, :, lanes],
                    come[j, :, 0, :, lanes],
                    inward[0, j, :, :, lanes],
                    inward[1, j, :, :, lanes],
                ):
                    rows[at : at + count, :] = part.reshape(count, LANES)
                    at += count
            for own_and_come in far_refs:
                count = own_and_come[j].shape[0] * GROUP
                rows[at : at + count, :] = own_and_come[j][:, :, lanes].reshape(count, LANES)
                at += count
    left_flat = [ref.reshape(left_rows * GROUP, LANES) for ref in left_refs]
    added = None
    for c in range(GROUP):
        left = [ref[pl.ds(c, left_rows, stride=GROUP), :] for ref in left_flat]
        right = [
            rows[pl.ds(n * height + c, pairs, stride=GROUP), :] for n in range(narrow * tiles)
        ]
        term = lax.dot_general(
            halves(jnp.concatenate(left, axis=1)),
            halves(jnp.concatenate(right, axis=1)),
            (((1,), (1,)), ((), ())),
            preferred_element_type=jnp.float32,
        )
        added = term if added is None else added + term
    total[...] += added

    @pl.when(step == pl.num_programs(0) - 1)
    def _():
        both = total[...]
        both = both[:left_rows] + both[left_rows:]
        turned = both.T
        value = turned[:pairs] + turned[pairs:]
        for ref in partial_refs:
            value = value + ref[...]
        if not last:
            out_ref[...] = value
        else:
            each = pairs // (INNER * len(masks))
            for n, mask in enumerate(masks):
                for i in range(INNER):
                    slot = n * INNER + i
                    out_ref[place_ref[3] ^ (INNER * mask + i)] = value[
                        slot * each : (slot + 1) * each
                    ]


def in_hbm(value):
    return pltpu.with_memory_space_constraint(value, pltpu.HBM)


def contract(place, integrals, near, far, partials, masks, start, count, last):
    left_rows, _, depth_all = integrals.shape
    narrow = len(far[0][1])
    depth = depth_all // narrow
    tiles = depth // LANES
    pairs = sum(INNER * value[0].shape[0] for _, value in near)
    pairs += sum(value[0].shape[0] for _, value in far)
    steps = count // GROUP
    first = start // GROUP

    def left_index(j, q, i, place):
        return (0, first + i, (place[4] ^ j) * tiles + q)

    in_specs = []
    for j in range(narrow):
        for q in range(tiles):
            in_specs.append(
                pl.BlockSpec((left_rows, GROUP, LANES), functools.partial(left_index, j, q))
            )
    for begins, value in near:
        each = value[0].shape[0]
        own, come, inward = [(start - at) // GROUP for at in begins]
        for _ in range(narrow):
            in_specs.append(
                pl.BlockSpec(
                    (each, 1, 1, GROUP, depth),
                    lambda i, place, own=own: (0, place[1], place[0], own + i, 0),
                )
            )
        in_specs.append(
            pl.BlockSpec(
                (narrow, each, 1, GROUP, depth),
                lambda i, place, come=come: (0, 0, place[1], come + i, 0),
            )
        )
        in_specs.append(
            pl.BlockSpec(
                (2, narrow, each, GROUP, depth),
                lambda i, place, inward=inward: (0, 0, 0, inward + i, 0),
            )
        )
    for begin, value in far:
        group = (start - begin) // GROUP
        for v in value:
            in_specs.append(
                pl.BlockSpec(
                    (v.shape[0], GROUP, depth), lambda i, place, group=group: (0, group + i, 0)
                )
            )
    for value in partials:
        in_specs.append(pl.BlockSpec(value.shape, lambda i, place: (0, 0)))
    if last:
        shape = (INNER * len(masks), pairs // (INNER * len(masks)), left_rows)
        out_spec = pl.BlockSpec(shape, lambda i, place: (0, 0, 0))
    else:
        shape = (pairs, left_rows)
        out_spec = pl.BlockSpec(shape, lambda i, place: (0, 0))
    return pl.pallas_call(
        functools.partial(
            contract_kernel, masks, len(near), len(far), narrow, len(partials), last
        ),
        out_shape=jax.ShapeDtypeStruct(shape, jnp.float32),
        grid_spec=pltpu.PrefetchScalarGridSpec(
            num_scalar_prefetch=1,
            grid=(steps,),
            in_specs=in_specs,
            out_specs=out_spec,
            scratch_shapes=[
                pltpu.VMEM((2 * left_rows, 2 * pairs), jnp.float32),
                pltpu.VMEM((pairs * GROUP * depth_all // LANES, LANES), jnp.float32),
            ],
        ),
        compiler_params=pltpu.CompilerParams(
            dimension_semantics=("arbitrary",), vmem_limit_bytes=32 << 20
        ),
        cost_estimate=pl.CostEstimate(
            flops=8 * left_rows * pairs * steps * GROUP * depth_all,
            bytes_accessed=4 * (left_rows + pairs) * steps * GROUP * depth_all,
            transcendentals=0,
        ),
    )(
        place,
        *([integrals] * (narrow * tiles)),
        *[in_hbm(v) for _, value in near for v in value],
        *[in_hbm(v) for _, value in far for v in value],
        *partials,
    )


def gather_kernel(copies, source_count, place_ref, *refs):
    sources = refs[:source_count]
    outs, sems = refs[source_count:-1], refs[-1]
    started = []
    for n, (source, source_at, out, out_at) in enumerate(copies):
        copy = pltpu.make_async_copy(
            sources[source].at[source_at(place_ref)], outs[out].at[out_at], sems.at[n]
        )
        copy.start()
        started.append(copy)
    for copy in started:
        copy.wait()


def gather(place, sources, shapes, copies):
    return pl.pallas_call(
        functools.partial(gather_kernel, copies, len(sources)),
        out_shape=[jax.ShapeDtypeStruct(shape, jnp.float32) for shape in shapes],
        grid_spec=pltpu.PrefetchScalarGridSpec(
            num_scalar_prefetch=1,
            grid=(),
            in_specs=[pl.BlockSpec(memory_space=pl.ANY)] * len(sources),
            out_specs=[pl.BlockSpec(memory_space=pltpu.VMEM)] * len(shapes),
            scratch_shapes=[pltpu.SemaphoreType.DMA((len(copies),))],
        ),
        compiler_params=pltpu.CompilerParams(vmem_limit_bytes=16 << 20),
        cost_estimate=pl.CostEstimate(flops=0, bytes_accessed=0, transcendentals=0),
    )(place, *sources)


ALL = slice(None)


class Plan:
    def __init__(self, place):
        self.place = place
        self.before = []
        self.reset()

    def reset(self):
        self.sources, self.shapes, self.copies = [], [], []

    def wait(self, *values):
        self.before.extend(values)

    def after(self, value):
        value, _ = lax.optimization_barrier((value, self.before))
        return value

    def new(self, *shape):
        self.shapes.append(shape)
        return len(self.shapes) - 1

    def put(self, out, out_at, value, source_at):
        index = next((n for n, v in enumerate(self.sources) if v is value), len(self.sources))
        if index == len(self.sources):
            self.sources.append(value)
        self.copies.append((index, source_at, out, out_at))

    def run(self):
        sources = list(self.sources)
        if self.before:
            sources, _ = lax.optimization_barrier((sources, self.before))
        made = list(gather(self.place, sources, self.shapes, self.copies))
        self.before = [made[0]]
        self.reset()
        return made


def shards(amplitudes, integrals, pair_index, window_virtuals, occ_energy, virt_energy):
    wide = lax.axis_size("wide")
    narrow = lax.axis_size("narrow")
    outer = wide // INNER
    place = lax.axis_index("wide")
    side = lax.axis_index("narrow")
    outer_place = place // INNER
    pairs_here, _, depth = amplitudes.shape
    rows_here, window, rows, depth_all = integrals.shape
    near_masks = list(range(outer // 2))
    far_masks = list(range(outer // 2, outer))
    blocks = amplitudes.reshape(pairs_here, outer, 2, 2, rows, depth)

    each = pairs_here
    far_count = len(far_masks)
    places = jnp.stack(
        [place & 1, (place >> 1) & 1, outer_place, place, side]
    ).astype(jnp.int32)
    plan = Plan(places)

    def outward(value, k):
        return swap(value, "wide", INNER * k)

    def sideways(value):
        return [value] + [swap(value, "narrow", j) for j in range(1, narrow)]

    half = GROUP * max(1, EARLY * rows // (8 * GROUP))
    early, late = (0, half), (half, rows - half)

    def core_step(sides):
        leave = plan.new(len(sides), each, 2, sides[0].shape[-2], depth)
        for j, v in enumerate(sides):
            plan.put(leave, (j,), v, lambda p: (ALL, ALL, 1 - p[0]))

    def high_step(sides, come, at=0, count=None):
        count = count or come.shape[-2]
        span = pl.ds(at, count)
        leave = plan.new(2, len(sides), each, count, depth)
        for j, v in enumerate(sides):
            plan.put(leave, (0, j), v, lambda p: (ALL, 1 - p[1], p[0], span))
        plan.put(leave, (1,), come, lambda p: (ALL, ALL, 1 - p[1], span))

    def cut(k, span):
        out = plan.new(each, 2, 2, span[1], depth)
        plan.put(out, (), blocks, lambda p: (ALL, p[2] ^ k, ALL, ALL, pl.ds(*span)))

    lead = far_masks[0]
    others = near_masks[1:]
    rest = [(k, early) for k in far_masks[1:]]
    rest += [(k, late) for k in others + far_masks]

    cut(lead, early)
    first = outward(plan.run()[0], lead)
    cut(0, (0, rows))
    offsets = [sum(span[1] for _, span in rest[:n]) for n in range(len(rest) + 1)]
    leave = plan.new(each, 2, offsets[-1], depth)
    for n, (k, span) in enumerate(rest):
        plan.put(
            leave,
            (ALL, ALL, pl.ds(offsets[n], span[1])),
            blocks,
            lambda p, k=k, span=span: (ALL, p[2] ^ k, ALL, 1 - p[0], pl.ds(*span)),
        )
    for k in others:
        cut(k, early)
    made = plan.run()
    side_early = [outward(v, k) for v, k in zip(made[2:], others)]
    home = sideways(made[0])
    rest_come = swap(made[1], "wide", 1)
    for n, (k, span) in enumerate(rest):
        leave = plan.new(2, each, span[1], depth)
        plan.put(
            leave,
            (0,),
            blocks,
            lambda p, k=k, span=span: (ALL, p[2] ^ k, 1 - p[1], p[0], pl.ds(*span)),
        )
        there = pl.ds(offsets[n], span[1])
        plan.put(leave, (1,), rest_come, lambda p, there=there: (ALL, 1 - p[1], there))
    rest_in = [swap(v, "wide", 2) for v in plan.run()]

    def rest_piece(k, span, part=None):
        n = rest.index((k, span))
        at, count = part or span
        inside = pl.ds(at - span[0], count)
        rows_here = pl.ds(at, count)
        out = plan.new(2, 2, each, count, depth)
        plan.put(out, (0, 0), blocks, lambda p: (ALL, p[2] ^ k, p[1], p[0], rows_here))
        there = pl.ds(offsets[n] + at - span[0], count)
        plan.put(out, (0, 1), rest_come, lambda p: (ALL, p[1], there))
        plan.put(out, (1,), rest_in[n], lambda p: (ALL, ALL, inside))

    last_spans = [late]
    if late[1] >= 2 * GROUP:
        tail = GROUP * (late[1] // (2 * GROUP))
        last_spans = [(half, late[1] - tail), (rows - tail, tail)]
    late_parts = [(k, late) for k in far_masks[:-1]] + [(far_masks[-1], part) for part in last_spans]
    far = {k: [] for k in others + far_masks}

    def across(k, begin, value):
        sides = sideways(value.reshape(INNER * each, -1, depth))
        far[k].append((begin, sides))
        return sides[1]

    def side_pieces(span):
        for k in others:
            rest_piece(k, span)
        return [(k, span[0], outward(v, k)) for k, v in zip(others, plan.run())] if others else []

    def crossing(pieces):
        plan.wait([v for _, _, v in pieces])
        return [across(k, begin, plan.after(v)) for k, begin, v in pieces]

    plan.wait(first, side_early, rest_in[: far_count - 1 + len(others)])
    sides = [sideways(plan.after(v)) for v in side_early]
    core_step([first])
    for k in far_masks[1:]:
        rest_piece(k, early)
    made = plan.run()
    going = [(k, 0, outward(v, k)) for k, v in zip(far_masks[1:], made[1:])]
    come = swap(made[0], "wide", 1)
    high_step([first], come)
    inward = swap(plan.run()[0], "wide", 2)
    plan.wait(rest_in)
    own = plan.new(2, 2, each, half, depth)
    plan.put(own, (0, 0), first, lambda p: (ALL, p[1], p[0]))
    plan.put(own, (0, 1), come, lambda p: (0, ALL, p[1]))
    plan.put(own, (1,), inward, lambda p: (ALL, 0))
    lead_own = plan.run()[0]
    plan.wait(home[1])
    crossed = [v[1] for v in sides]
    lead_crossed = across(lead, 0, lead_own)
    side_late = side_pieces(late)

    for k, part in late_parts:
        rest_piece(k, late, part)
    plan.wait([v for _, _, v in going])
    late_out = plan.run()
    later = [
        (k, late[0], outward(v, k)) for (k, _), v in zip(late_parts[: far_count - 1], late_out)
    ]
    plan.wait(crossed)
    crossed = crossing(going)
    for v in [home] + sides:
        core_step(v)
    comes = [swap(v, "wide", 1) for v in plan.run()]
    high_step(home, comes[0], *early)
    for v, come in zip(sides, comes[1:]):
        high_step(v, come)
    high_step(home, comes[0], *late)
    made = plan.run()
    inner = [swap(v, "wide", 2) for v in made[:-1]]
    plan.wait(lead_crossed)
    side_crossed = crossing(side_late)

    plan.wait(crossed, inner[0])
    home_late = swap(plan.after(made[-1]), "wide", 2)
    final = [(far_masks[-1], part) for part in last_spans]
    final_out = late_out[far_count - 1 :]
    plan.wait([v for _, _, v in later])
    ending = [
        (k, part[0], outward(plan.after(v), k)) for (k, part), v in zip(final[:1], final_out)
    ]
    crossed = crossing(later)

    flat_integrals = integrals.reshape(rows_here * window, rows, depth_all)
    partials = []
    near = [[((0, 0, 0), v + [c, i]) for v, c, i in zip([home] + sides, comes, inner)]]
    near.append([((0, 0, late[0]), home + [comes[0], home_late])])

    def multiply(h, span, last):
        pieces = [
            next(v for v in reversed(far[k]) if v[0] <= span[0])
            for k in (others if h else []) + far_masks
        ]
        value = contract(
            places,
            plan.after(flat_integrals),
            near[h],
            pieces,
            partials if last else [],
            near_masks + far_masks,
            *span,
            last,
        )
        plan.before = [value]
        partials.append(value)

    multiply(0, early, False)
    plan.wait(side_crossed)
    crossing(ending)
    for (k, part), v in zip(final[1:], final_out[1:]):
        ending = [(k, part[0], outward(plan.after(v), k))]
    if final[1:]:
        crossing(ending)
    for n, part in enumerate(last_spans):
        multiply(1, part, n == len(last_spans) - 1)
    value = partials[-1]

    sent = jnp.broadcast_to(value[:, None], (wide, narrow) + value.shape[1:])
    sent = sent.reshape((wide * narrow,) + value.shape[1:])
    got = lax.all_to_all(sent, ("wide", "narrow"), 0, 0, tiled=True)
    got = got.reshape(wide, narrow, pairs_here, rows_here, window)
    whole = jnp.sum(got, axis=0).transpose(0, 2, 3, 1).reshape(window, window, pairs_here)
    row_start = side * rows_here
    combined = whole + jnp.transpose(whole, (1, 0, 2))
    combined = lax.dynamic_slice_in_dim(combined, row_start, rows_here, 0)
    own_virtuals = lax.dynamic_slice_in_dim(window_virtuals, row_start, rows_here, 0)
    row_energy = lookup(virt_energy, own_virtuals)
    column_energy = lookup(virt_energy, window_virtuals)
    pair_energy = lookup(occ_energy, pair_index[:, 0]) + lookup(occ_energy, pair_index[:, 1])
    denominator = (
        pair_energy[None, None, :] - row_energy[:, None, None] - column_energy[None, :, None]
    )
    return combined / denominator


def solution(mesh):
    in_specs = (
        P("wide", None, "narrow"),
        P("narrow", None, "wide", None),
        P("wide", None),
        P(),
        P(),
        P(),
    )
    out_specs = P("narrow", None, "wide")
    return jax.shard_map(shards, mesh=mesh, in_specs=in_specs, out_specs=out_specs, check_vma=False)
```

time: 276 us -> 197 us (0.71)
  starting transfers between devices: 75.8 us -> 41.2 us
  waiting for transfers between devices: 130 us -> 108 us
  other arithmetic: 21.4 us -> 1.96 us
  local copies, waits for them, and re-layouts: 18.5 us -> 5.53 us
  Pallas kernels: 29.5 us -> 39.3 us
    ppermute x23 -> x27, starting transfers between devices: 72.5 us -> 38.4 us  [swap(): return lax.ppermute(value, axis, [(i, i ^ mask) for i in range(size)])]
    ppermute x23 -> x27, waiting for transfers between devices: 123 us -> 101 us  [swap(): return lax.ppermute(value, axis, [(i, i ^ mask) for i in range(size)])]
    another operation x16 -> x0, other arithmetic: 12.5 us -> none  [the longest x5 5.77 us: inner_exchange(): jnp.stack([pick(kept, 1 - high, x_axis), pick(come, 1 - high, x_axis)])]
    pallas_call x4 -> x13, Pallas kernels: 29.5 us -> 39.3 us  [the longest x3 28.4 us: contract(): pl.pallas_call(functools.partial(contract_kernel, masks, len(near), len(f...]
    squeeze x6 -> x0, other arithmetic: 6.93 us -> none  [the longest x4 4.91 us: pick(): return lax.dynamic_index_in_dim(value, index, axis, keepdims=False)]
    slice x2 -> x0, local copies, waits for them, and re-layouts: 6.7 us -> none  [the longest x1 4.82 us: shards(): blocks[..., first:, :]]
    another operation x6 -> x1, local copies, waits for them, and re-layouts: 5.33 us -> 0.08 us  [shards(): jnp.stack([place & 1, place >> 1 & 1, outer_place, place, side])]
    squeeze x2 -> x0, local copies, waits for them, and re-layouts: 4.69 us -> none  [pick(): return lax.dynamic_index_in_dim(value, index, axis, keepdims=False)]
  transfers between devices with their start and end apart: 24 -> 28, of which waited for: 11 -> 13; matrix products, arithmetic and copies ran while one was open for 12% -> 1% of each run, Pallas kernels for 9% -> 15%
where the time goes in v2:
time: 197 us; the launch traced here: 196 us
  waiting for transfers between devices  108 us (55%)
  starting transfers between devices  41.2 us (21%)
  Pallas kernels  39.3 us (20%)
  local copies, waits for them, and re-layouts  5.53 us (3%)
    ppermute x27, waiting for transfers between devices, swap(): return lax.ppermute(value, axis, [(i, i ^ mask) for i in range(size)])  101 us
    ppermute x27, starting transfers between devices, swap(): return lax.ppermute(value, axis, [(i, i ^ mask) for i in range(size)])  38.4 us
    pallas_call x3, Pallas kernels, contract(): pl.pallas_call(functools.partial(contract_kernel, masks, len(near), len(f...  28.4 us
    pallas_call x10, Pallas kernels, gather(): pl.pallas_call(functools.partial(gather_kernel, copies, len(sources)), ou...  10.8 us
    all_to_all x1, waiting for transfers between devices, shards(): got = lax.all_to_all(sent, ('wide', 'narrow'), 0, 0, tiled=True)  7.4 us
    unnamed x56, local copies, waits for them, and re-layouts  4.5 us
  transfers between devices with their start and end apart: 28, of which 13 were waited for; matrix products, arithmetic and copies ran while one was open for 1% of the time, Pallas kernels for 15%

profile of v2, /device:TPU:0, one launch (start us, length us, event | category | flops | bytes accessed | tf_op | source)
XLA Modules:
  0.0 196.4 jit_solution(2389992500055608683)
XLA Ops:
  0.1 2.8 %copy-done = f32[3,1024,512]{2,1,0:T(8,128)S(1)} copy-done((f32[3,1024,512]{2,1,0:T(8,128)S(1)}, f32[3,1024,512]{2,1,0:T(8,128)}, u32[]{:S(2)}) %copy-start) | copy-done | bytes 6291480
  5.0 2.6 %collective-permute-start.1 = (f32[3,2,2,32,512]{4,3,2,1,0:T(8,128)S(1)}, f32[3,2,2,32,512]{4,3,2,1,0:T(8,128)S(1)}, u32[]{:S(2)}, u32[]{:S(2)}) collective-permute-start(f32[3,2,2,32,512]{4,3,2,1,0:T(8,128)S(1)} %get-tuple-element.65), channel_id=1, source_target_pairs={{0,8},{2,10},{4,12},{6,14},{8,0},{10,2},{12,4},{14,6},{16,24},{18,... | collective-permute-start | bytes 2359304 | tf_op jit(solution)/shard_map/ppermute | solution.py:25
  7.7 2.6 %collective-permute-start.3 = (f32[3,2,2,32,512]{4,3,2,1,0:T(8,128)S(1)}, f32[3,2,2,32,512]{4,3,2,1,0:T(8,128)S(1)}, u32[]{:S(2)}, u32[]{:S(2)}) collective-permute-start(f32[3,2,2,32,512]{4,3,2,1,0:T(8,128)S(1)} %shard_map.64), channel_id=1, source_target_pairs={{0,16},{2,18},{4,20},{6,22},{8,24},{10,26},{12,28},{14,30},{16,0},... | collective-permute-start | bytes 2359304 | tf_op jit(solution)/shard_map/ppermute | solution.py:25
  10.3 1.5 collective-permute-start
  13.1 1.6 collective-permute-start.4
  15.2 27.3 %collective-permute-done.1.refs_2_.refs_3_.refs_12_ = f32[3,2,2,32,512]{4,3,2,1,0:T(8,128)S(1)} collective-permute-done((f32[3,2,2,32,512]{4,3,2,1,0:T(8,128)S(1)}, f32[3,2,2,32,512]{4,3,2,1,0:T(8,128)S(1)}, u32[]{:S(2)}, u32[]{:S(2)}) %collective-permute-start.1) | collective-permute-done | bytes 786464 | tf_op jit(solution)/shard_map/ppermute | solution.py:25
  42.5 2.5 %collective-permute-done.3.refs_0_ = f32[3,2,2,32,512]{4,3,2,1,0:T(8,128)S(1)} collective-permute-done((f32[3,2,2,32,512]{4,3,2,1,0:T(8,128)S(1)}, f32[3,2,2,32,512]{4,3,2,1,0:T(8,128)S(1)}, u32[]{:S(2)}, u32[]{:S(2)}) %collective-permute-start.3) | collective-permute-done | bytes 786464 | tf_op jit(solution)/shard_map/ppermute | solution.py:25
  46.2 1.6 collective-permute-start.7
  47.7 2.5 %collective-permute-start.11 = (f32[2,2,3,32,512]{4,3,2,1,0:T(8,128)S(1)}, f32[2,2,3,32,512]{4,3,2,1,0:T(8,128)S(1)}, u32[]{:S(2)}, u32[]{:S(2)}) collective-permute-start(f32[2,2,3,32,512]{4,3,2,1,0:T(8,128)S(1)} %get-tuple-element.87), channel_id=1, source_target_pairs={{0,24},{2,26},{4,28},{6,30},{8,16},{10,18},{12,20},{14,22},{16,8},... | collective-permute-start | bytes 2359304 | tf_op jit(solution)/shard_map/ppermute | solution.py:25
  50.2 1.5 collective-permute-start.6
  53.0 5.1 %collective-permute-done.7.refs_2_ = f32[2,3,32,512]{3,2,1,0:T(8,128)S(1)} collective-permute-done((f32[2,3,32,512]{3,2,1,0:T(8,128)S(1)}, f32[2,3,32,512]{3,2,1,0:T(8,128)S(1)}, u32[]{:S(2)}, u32[]{:S(2)}) %collective-permute-start.7) | collective-permute-done | bytes 393248 | tf_op jit(solution)/shard_map/ppermute | solution.py:25
  58.1 1.5 collective-permute-start.10
  59.6 6.9 %collective-permute-done.8.refs_3_ = f32[2,3,32,512]{3,2,1,0:T(8,128)S(1)} collective-permute-done((f32[2,3,32,512]{3,2,1,0:T(8,128)S(1)}, f32[2,3,32,512]{3,2,1,0:T(8,128)S(1)}, u32[]{:S(2)}, u32[]{:S(2)}) %collective-permute-start.8) | collective-permute-done | bytes 393248 | tf_op jit(solution)/shard_map/ppermute | solution.py:25
  66.6 8.0 %collective-permute-done.10.refs_2_ = f32[2,1,3,32,512]{4,3,2,1,0:T(8,128)S(1)} collective-permute-done((f32[2,1,3,32,512]{4,3,2,1,0:T(8,128)S(1)}, f32[2,1,3,32,512]{4,3,2,1,0:T(8,128)S(1)}, u32[]{:S(2)}, u32[]{:S(2)}) %collective-permute-start.10) | collective-permute-done | bytes 393248 | tf_op jit(solution)/shard_map/ppermute | solution.py:25
  79.3 1.5 collective-permute-start.14
  80.8 8.1 %collective-permute-start.15 = (f32[2,2,3,32,512]{4,3,2,1,0:T(8,128)S(1)}, f32[2,2,3,32,512]{4,3,2,1,0:T(8,128)S(1)}, u32[]{:S(2)}, u32[]{:S(2)}) collective-permute-start(f32[2,2,3,32,512]{4,3,2,1,0:T(8,128)S(1)} %shard_map.70), channel_id=1, source_target_pairs={{0,8},{2,10},{4,12},{6,14},{8,0},{10,2},{12,4},{14,6},{16,24},{18,... | collective-permute-start | bytes 2359304 | tf_op jit(solution)/shard_map/ppermute | solution.py:25
  89.5 2.2 %shard_map.73 = (f32[2,2,3,32,512]{4,3,2,1,0:T(8,128)S(1)}, f32[2,2,3,32,512]{4,3,2,1,0:T(8,128)S(1)}, f32[2,2,3,32,512]{4,3,2,1,0:T(8,128)}) custom-call(s32[5]{0:T(128)S(1)} %stack.23.place_ref, f32[3,2,2,64,512]{4,3,2,1,0:T(8,128)S(1)} %get-tuple-element.99.refs_0_.refs_8_, f32[3,2,2,64,512]{4,3,2,1,0:T(8,128)S(1)} %collective-permute-done.refs_1_.refs_9_, ...), custom_call_target="tpu_custom_call" | custom-call | tf_op jit(solution)/shard_map/pallas_call | solution.py:220
  92.3 7.3 %collective-permute-done.14.refs_17_ = f32[12,32,512]{2,1,0:T(8,128)S(1)} collective-permute-done((f32[12,32,512]{2,1,0:T(8,128)S(1)}, f32[12,32,512]{2,1,0:T(8,128)S(1)}, u32[]{:S(2)}, u32[]{:S(2)}) %collective-permute-start.14) | collective-permute-done | bytes 786464 | tf_op jit(solution)/shard_map/ppermute | solution.py:25
  99.7 1.5 collective-permute-start.19
  101.1 20.9 %collective-permute-done.15 = f32[2,2,3,32,512]{4,3,2,1,0:T(8,128)S(1)} collective-permute-done((f32[2,2,3,32,512]{4,3,2,1,0:T(8,128)S(1)}, f32[2,2,3,32,512]{4,3,2,1,0:T(8,128)S(1)}, u32[]{:S(2)}, u32[]{:S(2)}) %collective-permute-start.15) | collective-permute-done | bytes 786464 | tf_op jit(solution)/shard_map/ppermute | solution.py:25
  122.5 3.2 %collective-permute-done.18 = f32[2,2,3,32,512]{4,3,2,1,0:T(8,128)} collective-permute-done((f32[2,2,3,32,512]{4,3,2,1,0:T(8,128)S(1)}, f32[2,2,3,32,512]{4,3,2,1,0:T(8,128)}, u32[]{:S(2)}, u32[]{:S(2)}) %collective-permute-start.18) | collective-permute-done | bytes 786464 | tf_op jit(solution)/shard_map/ppermute | solution.py:25
  129.1 12.8 %shard_map.74.refs_18_ = f32[48,128]{1,0:T(8,128)S(1)} custom-call(s32[5]{0:T(128)S(1)} %stack.23.place_ref, f32[128,64,1024]{2,1,0:T(8,128)} %bitcast.39, f32[128,64,1024]{2,1,0:T(8,128)} %bitcast.40, f32[128,64,1024]{2,1,0:T(8,128)} %bitcast.41, f32[128,64,1024]{2,1,0:T(8,128)} %bitcast.42, f32[128,64,1024]{2,1,0:T(8,128)} %bitcast.43, ...), custom_call_target="tpu_custom_call" | custom-call | flops 1610612736 | bytes 23068672 | tf_op jit(solution)/shard_map/pallas_call | solution.py:173
  142.5 2.6 %collective-permute-start.22 = (f32[2,2,3,16,512]{4,3,2,1,0:T(8,128)S(1)}, f32[2,2,3,16,512]{4,3,2,1,0:T(8,128)}, u32[]{:S(2)}, u32[]{:S(2)}) collective-permute-start(f32[2,2,3,16,512]{4,3,2,1,0:T(8,128)S(1)} %get-tuple-element.113), channel_id=1, source_target_pairs={{0,24},{2,26},{4,28},{6,30},{8,16},{10,18},{12,20},{14,22},{16,8},... | collective-permute-start | bytes 1179656 | tf_op jit(solution)/shard_map/ppermute | solution.py:25
  145.1 1.5 collective-permute-start.25
  146.9 5.7 %collective-permute-done.22 = f32[2,2,3,16,512]{4,3,2,1,0:T(8,128)} collective-permute-done((f32[2,2,3,16,512]{4,3,2,1,0:T(8,128)S(1)}, f32[2,2,3,16,512]{4,3,2,1,0:T(8,128)}, u32[]{:S(2)}, u32[]{:S(2)}) %collective-permute-start.22) | collective-permute-done | bytes 393248 | tf_op jit(solution)/shard_map/ppermute | solution.py:25
  152.6 1.4 collective-permute-start.26
  154.9 4.5 %collective-permute-done.24.refs_15_ = f32[12,32,512]{2,1,0:T(8,128)S(1)} collective-permute-done((f32[12,32,512]{2,1,0:T(8,128)}, f32[12,32,512]{2,1,0:T(8,128)S(1)}, u32[]{:S(2)}, u32[]{:S(2)}) %collective-permute-start.24) | collective-permute-done | bytes 786464 | tf_op jit(solution)/shard_map/ppermute | solution.py:25
  159.3 8.5 %collective-permute-done.25.refs_17_ = f32[12,16,512]{2,1,0:T(8,128)} collective-permute-done((f32[12,16,512]{2,1,0:T(8,128)S(1)}, f32[12,16,512]{2,1,0:T(8,128)}, u32[]{:S(2)}, u32[]{:S(2)}) %collective-permute-start.25) | collective-permute-done | bytes 393248 | tf_op jit(solution)/shard_map/ppermute | solution.py:25
  167.9 7.8 %shard_map.75.refs_19_ = f32[48,128]{1,0:T(8,128)S(1)} custom-call(s32[5]{0:T(128)S(1)} %stack.23.place_ref, f32[128,64,1024]{2,1,0:T(8,128)} %bitcast.50, f32[128,64,1024]{2,1,0:T(8,128)} %bitcast.48, f32[128,64,1024]{2,1,0:T(8,128)} %bitcast.49, f32[128,64,1024]{2,1,0:T(8,128)} %bitcast.47, f32[128,64,1024]{2,1,0:T(8,128)} %bitcast.51, ...), custom_call_target="tpu_custom_call" | custom-call | flops 805306368 | bytes 11534336 | tf_op jit(solution)/shard_map/pallas_call | solution.py:173
  176.5 7.8 %shard_map.76 = f32[16,3,128]{2,1,0:T(4,128)S(1)} custom-call(s32[5]{0:T(128)S(1)} %stack.23.place_ref, f32[128,64,1024]{2,1,0:T(8,128)} %bitcast.55, f32[128,64,1024]{2,1,0:T(8,128)} %bitcast.56, f32[128,64,1024]{2,1,0:T(8,128)} %bitcast.57, f32[128,64,1024]{2,1,0:T(8,128)} %bitcast.58, f32[128,64,1024]{2,1,0:T(8,128)} %bitcast.59, ...), custom_call_target="tpu_custom_call" | custom-call | flops 805306368 | bytes 11534336 | tf_op jit(solution)/shard_map/pallas_call | solution.py:173
  184.9 2.8 %all-to-all-start = ((f32[32,3,128]{2,1,0:T(4,128)}), f32[32,3,128]{2,1,0:T(4,128)S(1)}, u32[]{:S(2)}, u32[]{:S(2)}) async-start(f32[32,3,128]{2,1,0:T(4,128)} %bitcast.13), calls=%async_computation | async-start | bytes 131072 | tf_op jit(solution)/shard_map/all_to_all | solution.py:475
  188.0 7.4 %all-to-all-done = f32[32,3,128]{2,1,0:T(4,128)S(1)} async-done(((f32[32,3,128]{2,1,0:T(4,128)}), f32[32,3,128]{2,1,0:T(4,128)S(1)}, u32[]{:S(2)}, u32[]{:S(2)}) %all-to-all-start) | async-done | bytes 49184 | tf_op jit(solution)/shard_map/all_to_all | solution.py:475
  (108 shorter events, 20.3 us)
Async XLA Ops:
  4.5 85.0 %copy-start.1 = (f32[3,2,2,64,512]{4,3,2,1,0:T(8,128)}, f32[3,2,2,64,512]{4,3,2,1,0:T(8,128)S(1)}, u32[]{:S(2)}) copy-start(f32[3,2,2,64,512]{4,3,2,1,0:T(8,128)S(1)} %get-tuple-element.99.refs_0_.refs_8_) | copy-start | bytes 4718596
  4.5 7.3 %collective-permute-start.2 = (f32[3,2,128,512]{3,2,1,0:T(8,128)S(1)}, f32[3,2,128,512]{3,2,1,0:T(8,128)S(1)}, u32[]{:S(2)}, u32[]{:S(2)}) collective-permute-start(f32[3,2,128,512]{3,2,1,0:T(8,128)S(1)} %get-tuple-element.66), channel_id=1, source_target_pairs={{0,2},{2,0},{4,6},{6,4},{8,10},{10,8},{12,14},{14,12},{16,18},{18,... | collective-permute-start | bytes 4718600 | tf_op jit(solution)/shard_map/ppermute | solution.py:25
  5.0 37.5 %collective-permute-start.1 = (f32[3,2,2,32,512]{4,3,2,1,0:T(8,128)S(1)}, f32[3,2,2,32,512]{4,3,2,1,0:T(8,128)S(1)}, u32[]{:S(2)}, u32[]{:S(2)}) collective-permute-start(f32[3,2,2,32,512]{4,3,2,1,0:T(8,128)S(1)} %get-tuple-element.65), channel_id=1, source_target_pairs={{0,8},{2,10},{4,12},{6,14},{8,0},{10,2},{12,4},{14,6},{16,24},{18,... | collective-permute-start | bytes 2359304 | tf_op jit(solution)/shard_map/ppermute | solution.py:25
  7.7 37.4 %collective-permute-start.3 = (f32[3,2,2,32,512]{4,3,2,1,0:T(8,128)S(1)}, f32[3,2,2,32,512]{4,3,2,1,0:T(8,128)S(1)}, u32[]{:S(2)}, u32[]{:S(2)}) collective-permute-start(f32[3,2,2,32,512]{4,3,2,1,0:T(8,128)S(1)} %shard_map.64), channel_id=1, source_target_pairs={{0,16},{2,18},{4,20},{6,22},{8,24},{10,26},{12,28},{14,30},{16,0},... | collective-permute-start | bytes 2359304 | tf_op jit(solution)/shard_map/ppermute | solution.py:25
  10.3 65.2 %collective-permute-start = (f32[3,2,2,64,512]{4,3,2,1,0:T(8,128)S(1)}, f32[3,2,2,64,512]{4,3,2,1,0:T(8,128)S(1)}, u32[]{:S(2)}, u32[]{:S(2)}) collective-permute-start(f32[3,2,2,64,512]{4,3,2,1,0:T(8,128)S(1)} %get-tuple-element.99.refs_0_.refs_8_), channel_id=1, source_target_pairs={{0,1},{1,0},{2,3},{3,2},{4,5},{5,4},{6,7},{7,6},{8,9},{9,8},{10,11... | collective-permute-start | bytes 4718600 | tf_op jit(solution)/shard_map/ppermute | solution.py:25
  11.8 63.7 %slice-start = ((s8[6291456]{0:T(1024)(128)(4,1)}), s8[4194304]{0:T(1024)(128)(4,1)S(1)}, s32[]{:S(2)}) async-start(s8[6291456]{0:T(1024)(128)(4,1)} %bitcast.33), calls=%async_computation.1 | async-start | bytes 8388608
  13.1 32.0 %collective-permute-start.4 = (f32[2,3,32,512]{3,2,1,0:T(8,128)S(1)}, f32[2,3,32,512]{3,2,1,0:T(8,128)S(1)}, u32[]{:S(2)}, u32[]{:S(2)}) collective-permute-start(f32[2,3,32,512]{3,2,1,0:T(8,128)S(1)} %get-tuple-element.69), channel_id=1, source_target_pairs={{0,4},{2,6},{4,0},{6,2},{8,12},{10,14},{12,8},{14,10},{16,20},{18,... | collective-permute-start | bytes 1179656 | tf_op jit(solution)/shard_map/ppermute | solution.py:25
  14.7 60.8 %slice-start.1 = ((s8[6291456]{0:T(1024)(128)(4,1)}), s8[2097152]{0:T(1024)(128)(4,1)S(1)}, s32[]{:S(2)}) async-start(s8[6291456]{0:T(1024)(128)(4,1)} %bitcast.33), calls=%async_computation.2 | async-start | bytes 4194304
  14.7 30.4 %collective-permute-start.5 = (f32[2,3,32,512]{3,2,1,0:T(8,128)S(1)}, f32[2,3,32,512]{3,2,1,0:T(8,128)S(1)}, u32[]{:S(2)}, u32[]{:S(2)}) collective-permute-start(f32[2,3,32,512]{3,2,1,0:T(8,128)S(1)} %get-tuple-element.70), channel_id=1, source_target_pairs={{0,4},{2,6},{4,0},{6,2},{8,12},{10,14},{12,8},{14,10},{16,20},{18,... | collective-permute-start | bytes 1179656 | tf_op jit(solution)/shard_map/ppermute | solution.py:25
  42.5 47.0 %copy-start.4 = (f32[3,2,2,32,512]{4,3,2,1,0:T(8,128)}, f32[3,2,2,32,512]{4,3,2,1,0:T(8,128)S(1)}, u32[]{:S(2)}) copy-start(f32[3,2,2,32,512]{4,3,2,1,0:T(8,128)S(1)} %collective-permute-done.1.refs_2_.refs_3_.refs_12_) | copy-start | bytes 2359300
  46.1 5.6 %collective-permute-start.9 = (f32[1,3,2,32,512]{4,3,2,1,0:T(8,128)S(1)}, f32[1,3,2,32,512]{4,3,2,1,0:T(8,128)S(1)}, u32[]{:S(2)}, u32[]{:S(2)}) collective-permute-start(f32[1,3,2,32,512]{4,3,2,1,0:T(8,128)S(1)} %get-tuple-element.78), channel_id=1, source_target_pairs={{0,2},{2,0},{4,6},{6,4},{8,10},{10,8},{12,14},{14,12},{16,18},{18,... | collective-permute-start | bytes 1179656 | tf_op jit(solution)/shard_map/ppermute | solution.py:25
  46.2 12.0 %collective-permute-start.7 = (f32[2,3,32,512]{3,2,1,0:T(8,128)S(1)}, f32[2,3,32,512]{3,2,1,0:T(8,128)S(1)}, u32[]{:S(2)}, u32[]{:S(2)}) collective-permute-start(f32[2,3,32,512]{3,2,1,0:T(8,128)S(1)} %get-tuple-element.72), channel_id=1, source_target_pairs={{0,4},{2,6},{4,0},{6,2},{8,12},{10,14},{12,8},{14,10},{16,20},{18,... | collective-permute-start | bytes 1179656 | tf_op jit(solution)/shard_map/ppermute | solution.py:25
  47.7 28.8 %collective-permute-start.11 = (f32[2,2,3,32,512]{4,3,2,1,0:T(8,128)S(1)}, f32[2,2,3,32,512]{4,3,2,1,0:T(8,128)S(1)}, u32[]{:S(2)}, u32[]{:S(2)}) collective-permute-start(f32[2,2,3,32,512]{4,3,2,1,0:T(8,128)S(1)} %get-tuple-element.87), channel_id=1, source_target_pairs={{0,24},{2,26},{4,28},{6,30},{8,16},{10,18},{12,20},{14,22},{16,8},... | collective-permute-start | bytes 2359304 | tf_op jit(solution)/shard_map/ppermute | solution.py:25
  50.2 27.6 %collective-permute-start.6 = (f32[3,2,2,32,512]{4,3,2,1,0:T(8,128)S(1)}, f32[3,2,2,32,512]{4,3,2,1,0:T(8,128)S(1)}, u32[]{:S(2)}, u32[]{:S(2)}) collective-permute-start(f32[3,2,2,32,512]{4,3,2,1,0:T(8,128)S(1)} %collective-permute-done.1.refs_2_.refs_3_.refs_12_), channel_id=1, source_target_pairs={{0,1},{1,0},{2,3},{3,2},{4,5},{5,4},{6,7},{7,6},{8,9},{9,8},{10,11... | collective-permute-start | bytes 2359304 | tf_op jit(solution)/shard_map/ppermute | solution.py:25
  51.7 14.9 %collective-permute-start.8 = (f32[2,3,32,512]{3,2,1,0:T(8,128)S(1)}, f32[2,3,32,512]{3,2,1,0:T(8,128)S(1)}, u32[]{:S(2)}, u32[]{:S(2)}) collective-permute-start(f32[2,3,32,512]{3,2,1,0:T(8,128)S(1)} %get-tuple-element.73), channel_id=1, source_target_pairs={{0,4},{2,6},{4,0},{6,2},{8,12},{10,14},{12,8},{14,10},{16,20},{18,... | collective-permute-start | bytes 1179656 | tf_op jit(solution)/shard_map/ppermute | solution.py:25
  58.1 16.4 %collective-permute-start.10 = (f32[2,1,3,32,512]{4,3,2,1,0:T(8,128)S(1)}, f32[2,1,3,32,512]{4,3,2,1,0:T(8,128)S(1)}, u32[]{:S(2)}, u32[]{:S(2)}) collective-permute-start(f32[2,1,3,32,512]{4,3,2,1,0:T(8,128)S(1)} %shard_map.68), channel_id=1, source_target_pairs={{0,4},{2,6},{4,0},{6,2},{8,12},{10,14},{12,8},{14,10},{16,20},{18,... | collective-permute-start | bytes 1179656 | tf_op jit(solution)/shard_map/ppermute | solution.py:25
  78.7 10.8 %collective-permute-start.12 = (f32[2,3,2,64,512]{4,3,2,1,0:T(8,128)S(1)}, f32[2,3,2,64,512]{4,3,2,1,0:T(8,128)S(1)}, u32[]{:S(2)}, u32[]{:S(2)}) collective-permute-start(f32[2,3,2,64,512]{4,3,2,1,0:T(8,128)S(1)} %get-tuple-element.97), channel_id=1, source_target_pairs={{0,2},{2,0},{4,6},{6,4},{8,10},{10,8},{12,14},{14,12},{16,18},{18,... | collective-permute-start | bytes 4718600 | tf_op jit(solution)/shard_map/ppermute | solution.py:25
  78.8 10.1 %collective-permute-start.13 = (f32[2,3,2,32,512]{4,3,2,1,0:T(8,128)S(1)}, f32[2,3,2,32,512]{4,3,2,1,0:T(8,128)S(1)}, u32[]{:S(2)}, u32[]{:S(2)}) collective-permute-start(f32[2,3,2,32,512]{4,3,2,1,0:T(8,128)S(1)} %get-tuple-element.98), channel_id=1, source_target_pairs={{0,2},{2,0},{4,6},{6,4},{8,10},{10,8},{12,14},{14,12},{16,18},{18,... | collective-permute-start | bytes 2359304 | tf_op jit(solution)/shard_map/ppermute | solution.py:25
  79.3 20.4 %collective-permute-start.14 = (f32[12,32,512]{2,1,0:T(8,128)S(1)}, f32[12,32,512]{2,1,0:T(8,128)S(1)}, u32[]{:S(2)}, u32[]{:S(2)}) collective-permute-start(f32[12,32,512]{2,1,0:T(8,128)S(1)} %bitcast.37), channel_id=1, source_target_pairs={{0,1},{1,0},{2,3},{3,2},{4,5},{5,4},{6,7},{7,6},{8,9},{9,8},{10,11... | collective-permute-start | bytes 2359304 | tf_op jit(solution)/shard_map/ppermute | solution.py:25
  80.8 41.2 %collective-permute-start.15 = (f32[2,2,3,32,512]{4,3,2,1,0:T(8,128)S(1)}, f32[2,2,3,32,512]{4,3,2,1,0:T(8,128)S(1)}, u32[]{:S(2)}, u32[]{:S(2)}) collective-permute-start(f32[2,2,3,32,512]{4,3,2,1,0:T(8,128)S(1)} %shard_map.70), channel_id=1, source_target_pairs={{0,8},{2,10},{4,12},{6,14},{8,0},{10,2},{12,4},{14,6},{16,24},{18,... | collective-permute-start | bytes 2359304 | tf_op jit(solution)/shard_map/ppermute | solution.py:25
  88.9 36.9 %collective-permute-start.18 = (f32[2,2,3,32,512]{4,3,2,1,0:T(8,128)S(1)}, f32[2,2,3,32,512]{4,3,2,1,0:T(8,128)}, u32[]{:S(2)}, u32[]{:S(2)}) collective-permute-start(f32[2,2,3,32,512]{4,3,2,1,0:T(8,128)S(1)} %get-tuple-element.92), channel_id=1, source_target_pairs={{0,16},{2,18},{4,20},{6,22},{8,24},{10,26},{12,28},{14,30},{16,0},... | collective-permute-start | bytes 2359304 | tf_op jit(solution)/shard_map/ppermute | solution.py:25
  88.9 33.6 %collective-permute-start.16 = (f32[12,32,512]{2,1,0:T(8,128)S(1)}, f32[12,32,512]{2,1,0:T(8,128)S(1)}, u32[]{:S(2)}, u32[]{:S(2)}) collective-permute-start(f32[12,32,512]{2,1,0:T(8,128)S(1)} %bitcast.66), channel_id=1, source_target_pairs={{0,1},{1,0},{2,3},{3,2},{4,5},{5,4},{6,7},{7,6},{8,9},{9,8},{10,11... | collective-permute-start | bytes 2359304 | tf_op jit(solution)/shard_map/ppermute | solution.py:25
  91.7 34.0 %collective-permute-start.17 = (f32[2,2,3,32,512]{4,3,2,1,0:T(8,128)S(1)}, f32[2,2,3,32,512]{4,3,2,1,0:T(8,128)S(1)}, u32[]{:S(2)}, u32[]{:S(2)}) collective-permute-start(f32[2,2,3,32,512]{4,3,2,1,0:T(8,128)S(1)} %get-tuple-element.105), channel_id=1, source_target_pairs={{0,4},{2,6},{4,0},{6,2},{8,12},{10,14},{12,8},{14,10},{16,20},{18,... | collective-permute-start | bytes 2359304 | tf_op jit(solution)/shard_map/ppermute | solution.py:25
  99.7 28.6 %collective-permute-start.19 = (f32[2,2,3,32,512]{4,3,2,1,0:T(8,128)S(1)}, f32[2,2,3,32,512]{4,3,2,1,0:T(8,128)S(1)}, u32[]{:S(2)}, u32[]{:S(2)}) collective-permute-start(f32[2,2,3,32,512]{4,3,2,1,0:T(8,128)S(1)} %get-tuple-element.108), channel_id=1, source_target_pairs={{0,4},{2,6},{4,0},{6,2},{8,12},{10,14},{12,8},{14,10},{16,20},{18,... | collective-permute-start | bytes 2359304 | tf_op jit(solution)/shard_map/ppermute | solution.py:25
  122.0 20.5 %collective-permute-start.20 = (f32[12,32,512]{2,1,0:T(8,128)S(1)}, f32[12,32,512]{2,1,0:T(8,128)S(1)}, u32[]{:S(2)}, u32[]{:S(2)}) collective-permute-start(f32[12,32,512]{2,1,0:T(8,128)S(1)} %bitcast.63), channel_id=1, source_target_pairs={{0,1},{1,0},{2,3},{3,2},{4,5},{5,4},{6,7},{7,6},{8,9},{9,8},{10,11... | collective-permute-start | bytes 2359304 | tf_op jit(solution)/shard_map/ppermute | solution.py:25
  125.8 16.7 %collective-permute-start.21 = (f32[2,2,3,16,512]{4,3,2,1,0:T(8,128)S(1)}, f32[2,2,3,16,512]{4,3,2,1,0:T(8,128)S(1)}, u32[]{:S(2)}, u32[]{:S(2)}) collective-permute-start(f32[2,2,3,16,512]{4,3,2,1,0:T(8,128)S(1)} %get-tuple-element.111), channel_id=1, source_target_pairs={{0,24},{2,26},{4,28},{6,30},{8,16},{10,18},{12,20},{14,22},{16,8},... | collective-permute-start | bytes 1179656 | tf_op jit(solution)/shard_map/ppermute | solution.py:25
  127.1 27.8 %collective-permute-start.23 = (f32[2,2,3,32,512]{4,3,2,1,0:T(8,128)}, f32[2,2,3,32,512]{4,3,2,1,0:T(8,128)S(1)}, u32[]{:S(2)}, u32[]{:S(2)}) collective-permute-start(f32[2,2,3,32,512]{4,3,2,1,0:T(8,128)} %get-tuple-element.116), channel_id=1, source_target_pairs={{0,4},{2,6},{4,0},{6,2},{8,12},{10,14},{12,8},{14,10},{16,20},{18,... | collective-permute-start | bytes 2359304 | tf_op jit(solution)/shard_map/ppermute | solution.py:25
  127.7 31.7 %collective-permute-start.24 = (f32[12,32,512]{2,1,0:T(8,128)}, f32[12,32,512]{2,1,0:T(8,128)S(1)}, u32[]{:S(2)}, u32[]{:S(2)}) collective-permute-start(f32[12,32,512]{2,1,0:T(8,128)} %bitcast.10.refs_14_), channel_id=1, source_target_pairs={{0,1},{1,0},{2,3},{3,2},{4,5},{5,4},{6,7},{7,6},{8,9},{9,8},{10,11... | collective-permute-start | bytes 2359304 | tf_op jit(solution)/shard_map/ppermute | solution.py:25
  142.5 10.1 %collective-permute-start.22 = (f32[2,2,3,16,512]{4,3,2,1,0:T(8,128)S(1)}, f32[2,2,3,16,512]{4,3,2,1,0:T(8,128)}, u32[]{:S(2)}, u32[]{:S(2)}) collective-permute-start(f32[2,2,3,16,512]{4,3,2,1,0:T(8,128)S(1)} %get-tuple-element.113), channel_id=1, source_target_pairs={{0,24},{2,26},{4,28},{6,30},{8,16},{10,18},{12,20},{14,22},{16,8},... | collective-permute-start | bytes 1179656 | tf_op jit(solution)/shard_map/ppermute | solution.py:25
  145.1 22.8 %collective-permute-start.25 = (f32[12,16,512]{2,1,0:T(8,128)S(1)}, f32[12,16,512]{2,1,0:T(8,128)}, u32[]{:S(2)}, u32[]{:S(2)}) collective-permute-start(f32[12,16,512]{2,1,0:T(8,128)S(1)} %bitcast.68), channel_id=1, source_target_pairs={{0,1},{1,0},{2,3},{3,2},{4,5},{5,4},{6,7},{7,6},{8,9},{9,8},{10,11... | collective-permute-start | bytes 1179656 | tf_op jit(solution)/shard_map/ppermute | solution.py:25
  152.6 23.1 %collective-permute-start.26 = (f32[12,16,512]{2,1,0:T(8,128)}, f32[12,16,512]{2,1,0:T(8,128)S(1)}, u32[]{:S(2)}, u32[]{:S(2)}) collective-permute-start(f32[12,16,512]{2,1,0:T(8,128)} %bitcast.12.refs_16_), channel_id=1, source_target_pairs={{0,1},{1,0},{2,3},{3,2},{4,5},{5,4},{6,7},{7,6},{8,9},{9,8},{10,11... | collective-permute-start | bytes 1179656 | tf_op jit(solution)/shard_map/ppermute | solution.py:25
  184.9 10.5 %all-to-all-start = ((f32[32,3,128]{2,1,0:T(4,128)}), f32[32,3,128]{2,1,0:T(4,128)S(1)}, u32[]{:S(2)}, u32[]{:S(2)}) async-start(f32[32,3,128]{2,1,0:T(4,128)} %bitcast.13), calls=%async_computation | async-start | bytes 131072 | tf_op jit(solution)/shard_map/all_to_all | solution.py:475
  (24 other events, 306.5 us)

commit v3 on v2

--- a/solution.py
+++ b/solution.py
@@ -104,9 +104,9 @@
             for n, mask in enumerate(masks):
                 for i in range(INNER):
                     slot = n * INNER + i
-                    out_ref[place_ref[3] ^ (INNER * mask + i)] = value[
-                        slot * each : (slot + 1) * each
-                    ]
+                    piece = value[slot * each : (slot + 1) * each]
+                    for j in range(narrow):
+                        out_ref[place_ref[3] ^ (INNER * mask + i), j] = piece
 
 
 def in_hbm(value):
@@ -165,8 +165,8 @@
     for value in partials:
         in_specs.append(pl.BlockSpec(value.shape, lambda i, place: (0, 0)))
     if last:
-        shape = (INNER * len(masks), pairs // (INNER * len(masks)), left_rows)
-        out_spec = pl.BlockSpec(shape, lambda i, place: (0, 0, 0))
+        shape = (INNER * len(masks), narrow, pairs // (INNER * len(masks)), left_rows)
+        out_spec = pl.BlockSpec(shape, lambda i, place: (0, 0, 0, 0))
     else:
         shape = (pairs, left_rows)
         out_spec = pl.BlockSpec(shape, lambda i, place: (0, 0))
@@ -197,7 +197,7 @@
         place,
         *([integrals] * (narrow * tiles)),
         *[in_hbm(v) for _, value in near for v in value],
-        *[in_hbm(v) for _, value in far for v in value],
+        *[v for _, value in far for v in value],
         *partials,
     )
 
@@ -216,14 +216,17 @@
         copy.wait()
 
 
-def gather(place, sources, shapes, copies):
+def gather(place, sources, shapes, copies, pinned):
     return pl.pallas_call(
         functools.partial(gather_kernel, copies, len(sources)),
         out_shape=[jax.ShapeDtypeStruct(shape, jnp.float32) for shape in shapes],
         grid_spec=pltpu.PrefetchScalarGridSpec(
             num_scalar_prefetch=1,
             grid=(),
-            in_specs=[pl.BlockSpec(memory_space=pl.ANY)] * len(sources),
+            in_specs=[
+                pl.BlockSpec(memory_space=pltpu.HBM if n in pinned else pl.ANY)
+                for n in range(len(sources))
+            ],
             out_specs=[pl.BlockSpec(memory_space=pltpu.VMEM)] * len(shapes),
             scratch_shapes=[pltpu.SemaphoreType.DMA((len(copies),))],
         ),
@@ -236,8 +239,9 @@
 
 
 class Plan:
-    def __init__(self, place):
+    def __init__(self, place, large):
         self.place = place
+        self.large = large
         self.before = []
         self.reset()
 
@@ -263,9 +267,11 @@
 
     def run(self):
         sources = list(self.sources)
+        pinned = [n for n, v in enumerate(sources) if v is self.large]
         if self.before:
             sources, _ = lax.optimization_barrier((sources, self.before))
-        made = list(gather(self.place, sources, self.shapes, self.copies))
+        sources = [in_hbm(v) if n in pinned else v for n, v in enumerate(sources)]
+        made = list(gather(self.place, sources, self.shapes, self.copies, pinned))
         self.before = [made[0]]
         self.reset()
         return made
@@ -282,6 +288,14 @@
     rows_here, window, rows, depth_all = integrals.shape
     near_masks = list(range(outer // 2))
     far_masks = list(range(outer // 2, outer))
+    row_start = side * rows_here
+    own_virtuals = lax.dynamic_slice_in_dim(window_virtuals, row_start, rows_here, 0)
+    row_energy = lookup(virt_energy, own_virtuals)
+    column_energy = lookup(virt_energy, window_virtuals)
+    pair_energy = lookup(occ_energy, pair_index[:, 0]) + lookup(occ_energy, pair_index[:, 1])
+    denominator = (
+        pair_energy[None, None, :] - row_energy[:, None, None] - column_energy[None, :, None]
+    )
     blocks = amplitudes.reshape(pairs_here, outer, 2, 2, rows, depth)
 
     each = pairs_here
@@ -289,7 +303,7 @@
     places = jnp.stack(
         [place & 1, (place >> 1) & 1, outer_place, place, side]
     ).astype(jnp.int32)
-    plan = Plan(places)
+    plan = Plan(places, blocks)
 
     def outward(value, k):
         return swap(value, "wide", INNER * k)
@@ -340,16 +354,22 @@
     side_early = [outward(v, k) for v, k in zip(made[2:], others)]
     home = sideways(made[0])
     rest_come = swap(made[1], "wide", 1)
+    single = len(rest) - far_count
     for n, (k, span) in enumerate(rest):
-        leave = plan.new(2, each, span[1], depth)
+        there = pl.ds(offsets[n], span[1])
+        if n < single:
+            leave, at = plan.new(2, each, span[1], depth), ()
+        else:
+            if n == single:
+                leave = plan.new(2, far_count, each, span[1], depth)
+            at = (n - single,)
         plan.put(
             leave,
-            (0,),
+            (0,) + at,
             blocks,
             lambda p, k=k, span=span: (ALL, p[2] ^ k, 1 - p[1], p[0], pl.ds(*span)),
         )
-        there = pl.ds(offsets[n], span[1])
-        plan.put(leave, (1,), rest_come, lambda p, there=there: (ALL, 1 - p[1], there))
+        plan.put(leave, (1,) + at, rest_come, lambda p, there=there: (ALL, 1 - p[1], there))
     rest_in = [swap(v, "wide", 2) for v in plan.run()]
 
     def rest_piece(k, span, part=None):
@@ -361,7 +381,10 @@
         plan.put(out, (0, 0), blocks, lambda p: (ALL, p[2] ^ k, p[1], p[0], rows_here))
         there = pl.ds(offsets[n] + at - span[0], count)
         plan.put(out, (0, 1), rest_come, lambda p: (ALL, p[1], there))
-        plan.put(out, (1,), rest_in[n], lambda p: (ALL, ALL, inside))
+        if n < single:
+            plan.put(out, (1,), rest_in[n], lambda p: (ALL, ALL, inside))
+        else:
+            plan.put(out, (1,), rest_in[-1], lambda p: (ALL, n - single, ALL, inside))
 
     last_spans = [late]
     if late[1] >= 2 * GROUP:
@@ -375,26 +398,25 @@
         far[k].append((begin, sides))
         return sides[1]
 
-    def side_pieces(span):
-        for k in others:
-            rest_piece(k, span)
-        return [(k, span[0], outward(v, k)) for k, v in zip(others, plan.run())] if others else []
-
     def crossing(pieces):
         plan.wait([v for _, _, v in pieces])
         return [across(k, begin, plan.after(v)) for k, begin, v in pieces]
 
-    plan.wait(first, side_early, rest_in[: far_count - 1 + len(others)])
+    plan.wait(side_early, rest_in[: far_count - 1 + len(others)], home[1])
     sides = [sideways(plan.after(v)) for v in side_early]
-    core_step([first])
     for k in far_masks[1:]:
         rest_piece(k, early)
+    for k in others:
+        rest_piece(k, late)
     made = plan.run()
-    going = [(k, 0, outward(v, k)) for k, v in zip(far_masks[1:], made[1:])]
-    come = swap(made[0], "wide", 1)
+    going = [(k, 0, outward(v, k)) for k, v in zip(far_masks[1:], made)]
+    side_late = [(k, late[0], outward(v, k)) for k, v in zip(others, made[far_count - 1 :])]
+    plan.wait(first)
+    core_step([first])
+    come = swap(plan.run()[0], "wide", 1)
     high_step([first], come)
     inward = swap(plan.run()[0], "wide", 2)
-    plan.wait(rest_in)
+    plan.wait(denominator)
     own = plan.new(2, 2, each, half, depth)
     plan.put(own, (0, 0), first, lambda p: (ALL, p[1], p[0]))
     plan.put(own, (0, 1), come, lambda p: (0, ALL, p[1]))
@@ -403,7 +425,6 @@
     plan.wait(home[1])
     crossed = [v[1] for v in sides]
     lead_crossed = across(lead, 0, lead_own)
-    side_late = side_pieces(late)
 
     for k, part in late_parts:
         rest_piece(k, late, part)
@@ -413,6 +434,8 @@
         (k, late[0], outward(v, k)) for (k, _), v in zip(late_parts[: far_count - 1], late_out)
     ]
     plan.wait(crossed)
+    side_crossed = crossing(side_late)
+    plan.wait(lead_crossed)
     crossed = crossing(going)
     for v in [home] + sides:
         core_step(v)
@@ -423,8 +446,6 @@
     high_step(home, comes[0], *late)
     made = plan.run()
     inner = [swap(v, "wide", 2) for v in made[:-1]]
-    plan.wait(lead_crossed)
-    side_crossed = crossing(side_late)
 
     plan.wait(crossed, inner[0])
     home_late = swap(plan.after(made[-1]), "wide", 2)
@@ -459,32 +480,25 @@
         plan.before = [value]
         partials.append(value)
 
-    multiply(0, early, False)
+    part = GROUP * max(1, half // (2 * GROUP))
+    multiply(0, (0, part), False)
+    for (k, span), v in zip(final[1:], final_out[1:]):
+        ending.append((k, span[0], outward(plan.after(v), k)))
+    if part < half:
+        multiply(0, (part, half - part), False)
     plan.wait(side_crossed)
-    crossing(ending)
-    for (k, part), v in zip(final[1:], final_out[1:]):
-        ending = [(k, part[0], outward(plan.after(v), k))]
-    if final[1:]:
-        crossing(ending)
-    for n, part in enumerate(last_spans):
-        multiply(1, part, n == len(last_spans) - 1)
+    for n in range(len(ending)):
+        crossing(ending[n : n + 1])
+    for n, span in enumerate(last_spans):
+        multiply(1, span, n == len(last_spans) - 1)
     value = partials[-1]
 
-    sent = jnp.broadcast_to(value[:, None], (wide, narrow) + value.shape[1:])
-    sent = sent.reshape((wide * narrow,) + value.shape[1:])
+    sent = value.reshape((wide * narrow,) + value.shape[2:])
     got = lax.all_to_all(sent, ("wide", "narrow"), 0, 0, tiled=True)
     got = got.reshape(wide, narrow, pairs_here, rows_here, window)
     whole = jnp.sum(got, axis=0).transpose(0, 2, 3, 1).reshape(window, window, pairs_here)
-    row_start = side * rows_here
     combined = whole + jnp.transpose(whole, (1, 0, 2))
     combined = lax.dynamic_slice_in_dim(combined, row_start, rows_here, 0)
-    own_virtuals = lax.dynamic_slice_in_dim(window_virtuals, row_start, rows_here, 0)
-    row_energy = lookup(virt_energy, own_virtuals)
-    column_energy = lookup(virt_energy, window_virtuals)
-    pair_energy = lookup(occ_energy, pair_index[:, 0]) + lookup(occ_energy, pair_index[:, 1])
-    denominator = (
-        pair_energy[None, None, :] - row_energy[:, None, None] - column_energy[None, :, None]
-    )
     return combined / denominator
 
 

time: 197 us -> 194 us (0.985)
  Pallas kernels: 39.3 us -> 47.4 us
  starting transfers between devices: 41.2 us -> 33.4 us
  local copies, waits for them, and re-layouts: 5.53 us -> 1.37 us
    ppermute x27 -> x26, starting transfers between devices: 38.4 us -> 29.3 us  [swap(): return lax.ppermute(value, axis, [(i, i ^ mask) for i in range(size)])]
    pallas_call x10, Pallas kernels: 10.8 us -> 16.1 us  [gather(): pl.pallas_call(functools.partial(gather_kernel, copies, len(sources)), ou...]
    unnamed x56 -> x30, local copies, waits for them, and re-layouts: 4.5 us -> 0.97 us
    pallas_call x3 -> x4, Pallas kernels: 28.4 us -> 31.4 us  [contract(): pl.pallas_call(functools.partial(contract_kernel, masks, len(near), len(f...]
    ppermute x27 -> x26, waiting for transfers between devices: 101 us -> 102 us  [swap(): return lax.ppermute(value, axis, [(i, i ^ mask) for i in range(size)])]
  transfers between devices with their start and end apart: 28 -> 27, of which waited for: 13 -> 13; matrix products, arithmetic and copies ran while one was open for 1% -> 1% of each run, Pallas kernels for 15% -> 17%
where the time goes in v3:
time: 194 us
  waiting for transfers between devices  109 us (56%)
  Pallas kernels  47.4 us (24%)
  starting transfers between devices  33.4 us (17%)
  other arithmetic  1.96 us (1%)
    ppermute x26, waiting for transfers between devices, swap(): return lax.ppermute(value, axis, [(i, i ^ mask) for i in range(size)])  102 us
    pallas_call x4, Pallas kernels, contract(): pl.pallas_call(functools.partial(contract_kernel, masks, len(near), len(f...  31.4 us
    ppermute x26, starting transfers between devices, swap(): return lax.ppermute(value, axis, [(i, i ^ mask) for i in range(size)])  29.3 us
    pallas_call x10, Pallas kernels, gather(): pl.pallas_call(functools.partial(gather_kernel, copies, len(sources)), ou...  16.1 us
    all_to_all x1, waiting for transfers between devices, shards(): got = lax.all_to_all(sent, ('wide', 'narrow'), 0, 0, tiled=True)  7.38 us
    all_to_all x1, starting transfers between devices, shards(): got = lax.all_to_all(sent, ('wide', 'narrow'), 0, 0, tiled=True)  4.16 us
  transfers between devices with their start and end apart: 27, of which 13 were waited for; matrix products, arithmetic and copies ran while one was open for 1% of the time, Pallas kernels for 17%

profile of v3, /device:TPU:0, one launch (start us, length us, event | category | flops | bytes accessed | tf_op | source)
XLA Modules:
  0.0 193.7 jit_solution(16278068507208672943)
XLA Ops:
  0.1 1.7 shard_map.64
  1.8 2.7 %shard_map.65 = (f32[3,2,2,64,512]{4,3,2,1,0:T(8,128)S(1)}, f32[3,2,128,512]{3,2,1,0:T(8,128)S(1)}, f32[3,2,2,32,512]{4,3,2,1,0:T(8,128)S(1)}) custom-call(s32[5]{0:T(128)S(1)} %stack.23.place_ref, f32[3,4,2,2,64,512]{5,4,3,2,1,0:T(8,128)} %bitcast.71), custom_call_target="tpu_custom_call" | custom-call | tf_op jit(solution)/shard_map/pallas_call | solution.py:220
  5.0 2.6 %collective-permute-start = (f32[3,2,2,64,512]{4,3,2,1,0:T(8,128)S(1)}, f32[3,2,2,64,512]{4,3,2,1,0:T(8,128)S(1)}, u32[]{:S(2)}, u32[]{:S(2)}) collective-permute-start(f32[3,2,2,64,512]{4,3,2,1,0:T(8,128)S(1)} %get-tuple-element.92.refs_0_.refs_8_), channel_id=1, source_target_pairs={{0,1},{1,0},{2,3},{3,2},{4,5},{5,4},{6,7},{7,6},{8,9},{9,8},{10,11... | collective-permute-start | bytes 4718600 | tf_op jit(solution)/shard_map/ppermute | solution.py:25
  7.6 1.6 collective-permute-start.1
  9.2 2.6 %collective-permute-start.7 = (f32[3,2,2,32,512]{4,3,2,1,0:T(8,128)S(1)}, f32[3,2,2,32,512]{4,3,2,1,0:T(8,128)S(1)}, u32[]{:S(2)}, u32[]{:S(2)}) collective-permute-start(f32[3,2,2,32,512]{4,3,2,1,0:T(8,128)S(1)} %shard_map.64), channel_id=1, source_target_pairs={{0,16},{2,18},{4,20},{6,22},{8,24},{10,26},{12,28},{14,30},{16,0},... | collective-permute-start | bytes 2359304 | tf_op jit(solution)/shard_map/ppermute | solution.py:25
  11.8 1.9 shard_map.66
  13.7 1.6 collective-permute-start.4
  15.7 28.2 %collective-permute-done.1.refs_2_.refs_3_.refs_12_ = f32[3,2,2,32,512]{4,3,2,1,0:T(8,128)S(1)} collective-permute-done((f32[3,2,2,32,512]{4,3,2,1,0:T(8,128)S(1)}, f32[3,2,2,32,512]{4,3,2,1,0:T(8,128)S(1)}, u32[]{:S(2)}, u32[]{:S(2)}) %collective-permute-start.1) | collective-permute-done | bytes 786464 | tf_op jit(solution)/shard_map/ppermute | solution.py:25
  44.0 1.9 shard_map.67
  47.0 1.7 collective-permute-done.8.refs_1_
  49.4 1.6 collective-permute-start.9
  51.5 2.5 %collective-permute-start.10 = (f32[2,2,3,32,512]{4,3,2,1,0:T(8,128)S(1)}, f32[2,2,3,32,512]{4,3,2,1,0:T(8,128)S(1)}, u32[]{:S(2)}, u32[]{:S(2)}) collective-permute-start(f32[2,2,3,32,512]{4,3,2,1,0:T(8,128)S(1)} %get-tuple-element.74), channel_id=1, source_target_pairs={{0,24},{2,26},{4,28},{6,30},{8,16},{10,18},{12,20},{14,22},{16,8},... | collective-permute-start | bytes 2359304 | tf_op jit(solution)/shard_map/ppermute | solution.py:25
  55.0 6.4 %collective-permute-done.9.refs_2_ = f32[2,1,3,32,512]{4,3,2,1,0:T(8,128)S(1)} collective-permute-done((f32[2,1,3,32,512]{4,3,2,1,0:T(8,128)S(1)}, f32[2,1,3,32,512]{4,3,2,1,0:T(8,128)S(1)}, u32[]{:S(2)}, u32[]{:S(2)}) %collective-permute-start.9) | collective-permute-done | bytes 393248 | tf_op jit(solution)/shard_map/ppermute | solution.py:25
  63.0 14.5 %collective-permute-done.6.refs_2_ = f32[2,2,3,32,512]{4,3,2,1,0:T(8,128)S(1)} collective-permute-done((f32[2,2,3,32,512]{4,3,2,1,0:T(8,128)S(1)}, f32[2,2,3,32,512]{4,3,2,1,0:T(8,128)S(1)}, u32[]{:S(2)}, u32[]{:S(2)}) %collective-permute-start.6) | collective-permute-done | bytes 786464 | tf_op jit(solution)/shard_map/ppermute | solution.py:25
  77.5 2.6 %shard_map.71 = (f32[2,2,3,32,512]{4,3,2,1,0:T(8,128)S(1)}, f32[2,2,3,16,512]{4,3,2,1,0:T(8,128)}, f32[2,2,3,16,512]{4,3,2,1,0:T(8,128)S(1)}) custom-call(s32[5]{0:T(128)S(1)} %stack.23.place_ref, f32[3,4,2,2,64,512]{5,4,3,2,1,0:T(8,128)} %bitcast.74, f32[3,2,128,512]{3,2,1,0:T(8,128)S(1)} %collective-permute-done.2.refs_1_, ...), custom_call_target="tpu_custom_call" | custom-call | tf_op jit(solution)/shard_map/pallas_call | solution.py:220
  80.1 9.3 %collective-permute-done.11 = f32[2,2,3,32,512]{4,3,2,1,0:T(8,128)} collective-permute-done((f32[2,2,3,32,512]{4,3,2,1,0:T(8,128)S(1)}, f32[2,2,3,32,512]{4,3,2,1,0:T(8,128)}, u32[]{:S(2)}, u32[]{:S(2)}) %collective-permute-start.11) | collective-permute-done | bytes 786464 | tf_op jit(solution)/shard_map/ppermute | solution.py:25
  91.0 1.6 collective-permute-start.17
  95.1 2.2 %shard_map.73 = (f32[2,2,3,32,512]{4,3,2,1,0:T(8,128)S(1)}, f32[2,2,3,32,512]{4,3,2,1,0:T(8,128)S(1)}, f32[2,2,3,32,512]{4,3,2,1,0:T(8,128)}) custom-call(s32[5]{0:T(128)S(1)} %stack.23.place_ref, f32[3,2,2,64,512]{4,3,2,1,0:T(8,128)S(1)} %get-tuple-element.92.refs_0_.refs_8_, f32[3,2,2,64,512]{4,3,2,1,0:T(8,128)S(1)} %collective-permute-done.refs_1_.refs_9_, ...), custom_call_target="tpu_custom_call" | custom-call | tf_op jit(solution)/shard_map/pallas_call | solution.py:220
  97.3 1.6 collective-permute-start.16
  100.5 27.9 %collective-permute-done.17 = f32[2,2,3,32,512]{4,3,2,1,0:T(8,128)} collective-permute-done((f32[2,2,3,32,512]{4,3,2,1,0:T(8,128)S(1)}, f32[2,2,3,32,512]{4,3,2,1,0:T(8,128)}, u32[]{:S(2)}, u32[]{:S(2)}) %collective-permute-start.17) | collective-permute-done | bytes 786464 | tf_op jit(solution)/shard_map/ppermute | solution.py:25
  128.4 1.5 collective-permute-start.20
  130.0 1.5 collective-permute-start.22
  132.5 2.2 %collective-permute-done.18.refs_15_ = f32[2,2,3,32,512]{4,3,2,1,0:T(8,128)S(1)} collective-permute-done((f32[2,2,3,32,512]{4,3,2,1,0:T(8,128)S(1)}, f32[2,2,3,32,512]{4,3,2,1,0:T(8,128)S(1)}, u32[]{:S(2)}, u32[]{:S(2)}) %collective-permute-start.18) | collective-permute-done | bytes 786464 | tf_op jit(solution)/shard_map/ppermute | solution.py:25
  135.6 7.6 %shard_map.74.refs_18_ = f32[48,128]{1,0:T(8,128)S(1)} custom-call(s32[5]{0:T(128)S(1)} %stack.23.place_ref, f32[128,64,1024]{2,1,0:T(8,128)} %bitcast.38, f32[128,64,1024]{2,1,0:T(8,128)} %bitcast.39, f32[128,64,1024]{2,1,0:T(8,128)} %bitcast.40, f32[128,64,1024]{2,1,0:T(8,128)} %bitcast.41, f32[128,64,1024]{2,1,0:T(8,128)} %bitcast.42, ...), custom_call_target="tpu_custom_call" | custom-call | flops 805306368 | bytes 11534336 | tf_op jit(solution)/shard_map/pallas_call | solution.py:173
  143.2 1.5 collective-permute-start.21
  144.8 7.7 %shard_map.75.refs_19_ = f32[48,128]{1,0:T(8,128)S(1)} custom-call(s32[5]{0:T(128)S(1)} %stack.23.place_ref, f32[128,64,1024]{2,1,0:T(8,128)} %bitcast.53, f32[128,64,1024]{2,1,0:T(8,128)} %bitcast.47, f32[128,64,1024]{2,1,0:T(8,128)} %bitcast.48, f32[128,64,1024]{2,1,0:T(8,128)} %bitcast.49, f32[128,64,1024]{2,1,0:T(8,128)} %bitcast.50, ...), custom_call_target="tpu_custom_call" | custom-call | flops 805306368 | bytes 11534336 | tf_op jit(solution)/shard_map/pallas_call | solution.py:173
  153.2 1.5 collective-permute-done.21
  156.5 8.2 %collective-permute-done.24.refs_17_ = f32[12,16,512]{2,1,0:T(8,128)S(1)} collective-permute-done((f32[12,16,512]{2,1,0:T(8,128)}, f32[12,16,512]{2,1,0:T(8,128)S(1)}, u32[]{:S(2)}, u32[]{:S(2)}) %collective-permute-start.24) | collective-permute-done | bytes 393248 | tf_op jit(solution)/shard_map/ppermute | solution.py:25
  164.8 7.7 %shard_map.76.refs_20_ = f32[48,128]{1,0:T(8,128)S(1)} custom-call(s32[5]{0:T(128)S(1)} %stack.23.place_ref, f32[128,64,1024]{2,1,0:T(8,128)} %bitcast.54, f32[128,64,1024]{2,1,0:T(8,128)} %bitcast.55, f32[128,64,1024]{2,1,0:T(8,128)} %bitcast.56, f32[128,64,1024]{2,1,0:T(8,128)} %bitcast.57, f32[128,64,1024]{2,1,0:T(8,128)} %bitcast.58, ...), custom_call_target="tpu_custom_call" | custom-call | flops 805306368 | bytes 11534336 | tf_op jit(solution)/shard_map/pallas_call | solution.py:173
  172.5 8.4 %shard_map.77 = f32[16,2,3,128]{3,2,1,0:T(4,128)} custom-call(s32[5]{0:T(128)S(1)} %stack.23.place_ref, f32[128,64,1024]{2,1,0:T(8,128)} %bitcast.62, f32[128,64,1024]{2,1,0:T(8,128)} %bitcast.63, f32[128,64,1024]{2,1,0:T(8,128)} %bitcast.64, f32[128,64,1024]{2,1,0:T(8,128)} %bitcast.65, f32[128,64,1024]{2,1,0:T(8,128)} %bitcast.66, ...), custom_call_target="tpu_custom_call" | custom-call | flops 805306368 | bytes 11534336 | tf_op jit(solution)/shard_map/pallas_call | solution.py:173
  180.9 4.2 %all-to-all-start = ((f32[32,3,128]{2,1,0:T(4,128)}), f32[32,3,128]{2,1,0:T(4,128)S(1)}, u32[]{:S(2)}, u32[]{:S(2)}) async-start(f32[32,3,128]{2,1,0:T(4,128)} %bitcast.15), calls=%async_computation | async-start | bytes 131072 | tf_op jit(solution)/shard_map/all_to_all | solution.py:497
  185.3 7.4 %all-to-all-done = f32[32,3,128]{2,1,0:T(4,128)S(1)} async-done(((f32[32,3,128]{2,1,0:T(4,128)}), f32[32,3,128]{2,1,0:T(4,128)S(1)}, u32[]{:S(2)}, u32[]{:S(2)}) %all-to-all-start) | async-done | bytes 49184 | tf_op jit(solution)/shard_map/all_to_all | solution.py:497
  (79 shorter events, 17.3 us)
Async XLA Ops:
  4.5 90.6 %copy-start = (f32[3,2,2,64,512]{4,3,2,1,0:T(8,128)}, f32[3,2,2,64,512]{4,3,2,1,0:T(8,128)S(1)}, u32[]{:S(2)}) copy-start(f32[3,2,2,64,512]{4,3,2,1,0:T(8,128)S(1)} %get-tuple-element.92.refs_0_.refs_8_) | copy-start | bytes 4718596
  4.5 7.3 %collective-permute-start.2 = (f32[3,2,128,512]{3,2,1,0:T(8,128)S(1)}, f32[3,2,128,512]{3,2,1,0:T(8,128)S(1)}, u32[]{:S(2)}, u32[]{:S(2)}) collective-permute-start(f32[3,2,128,512]{3,2,1,0:T(8,128)S(1)} %get-tuple-element.63), channel_id=1, source_target_pairs={{0,2},{2,0},{4,6},{6,4},{8,10},{10,8},{12,14},{14,12},{16,18},{18,... | collective-permute-start | bytes 4718600 | tf_op jit(solution)/shard_map/ppermute | solution.py:25
  5.0 38.9 %collective-permute-start = (f32[3,2,2,64,512]{4,3,2,1,0:T(8,128)S(1)}, f32[3,2,2,64,512]{4,3,2,1,0:T(8,128)S(1)}, u32[]{:S(2)}, u32[]{:S(2)}) collective-permute-start(f32[3,2,2,64,512]{4,3,2,1,0:T(8,128)S(1)} %get-tuple-element.92.refs_0_.refs_8_), channel_id=1, source_target_pairs={{0,1},{1,0},{2,3},{3,2},{4,5},{5,4},{6,7},{7,6},{8,9},{9,8},{10,11... | collective-permute-start | bytes 4718600 | tf_op jit(solution)/shard_map/ppermute | solution.py:25
  7.6 36.4 %collective-permute-start.1 = (f32[3,2,2,32,512]{4,3,2,1,0:T(8,128)S(1)}, f32[3,2,2,32,512]{4,3,2,1,0:T(8,128)S(1)}, u32[]{:S(2)}, u32[]{:S(2)}) collective-permute-start(f32[3,2,2,32,512]{4,3,2,1,0:T(8,128)S(1)} %get-tuple-element.62), channel_id=1, source_target_pairs={{0,8},{2,10},{4,12},{6,14},{8,0},{10,2},{12,4},{14,6},{16,24},{18,... | collective-permute-start | bytes 2359304 | tf_op jit(solution)/shard_map/ppermute | solution.py:25
  9.2 37.1 %collective-permute-start.7 = (f32[3,2,2,32,512]{4,3,2,1,0:T(8,128)S(1)}, f32[3,2,2,32,512]{4,3,2,1,0:T(8,128)S(1)}, u32[]{:S(2)}, u32[]{:S(2)}) collective-permute-start(f32[3,2,2,32,512]{4,3,2,1,0:T(8,128)S(1)} %shard_map.64), channel_id=1, source_target_pairs={{0,16},{2,18},{4,20},{6,22},{8,24},{10,26},{12,28},{14,30},{16,0},... | collective-permute-start | bytes 2359304 | tf_op jit(solution)/shard_map/ppermute | solution.py:25
  13.7 30.3 %collective-permute-start.4 = (f32[2,3,32,512]{3,2,1,0:T(8,128)S(1)}, f32[2,3,32,512]{3,2,1,0:T(8,128)S(1)}, u32[]{:S(2)}, u32[]{:S(2)}) collective-permute-start(f32[2,3,32,512]{3,2,1,0:T(8,128)S(1)} %get-tuple-element.67), channel_id=1, source_target_pairs={{0,4},{2,6},{4,0},{6,2},{8,12},{10,14},{12,8},{14,10},{16,20},{18,... | collective-permute-start | bytes 1179656 | tf_op jit(solution)/shard_map/ppermute | solution.py:25
  15.2 28.7 %collective-permute-start.3 = (f32[2,3,32,512]{3,2,1,0:T(8,128)S(1)}, f32[2,3,32,512]{3,2,1,0:T(8,128)S(1)}, u32[]{:S(2)}, u32[]{:S(2)}) collective-permute-start(f32[2,3,32,512]{3,2,1,0:T(8,128)S(1)} %get-tuple-element.66), channel_id=1, source_target_pairs={{0,4},{2,6},{4,0},{6,2},{8,12},{10,14},{12,8},{14,10},{16,20},{18,... | collective-permute-start | bytes 1179656 | tf_op jit(solution)/shard_map/ppermute | solution.py:25
  43.9 51.1 %copy-start.3 = (f32[3,2,2,32,512]{4,3,2,1,0:T(8,128)}, f32[3,2,2,32,512]{4,3,2,1,0:T(8,128)S(1)}, u32[]{:S(2)}) copy-start(f32[3,2,2,32,512]{4,3,2,1,0:T(8,128)S(1)} %collective-permute-done.1.refs_2_.refs_3_.refs_12_) | copy-start | bytes 2359300
  43.9 51.1 %copy-start.1 = (f32[3,2,2,64,512]{4,3,2,1,0:T(8,128)}, f32[3,2,2,64,512]{4,3,2,1,0:T(8,128)S(1)}, u32[]{:S(2)}) copy-start(f32[3,2,2,64,512]{4,3,2,1,0:T(8,128)S(1)} %collective-permute-done.refs_1_.refs_9_) | copy-start | bytes 4718596
  46.9 1.8 collective-permute-start.8
  49.4 12.0 %collective-permute-start.9 = (f32[2,1,3,32,512]{4,3,2,1,0:T(8,128)S(1)}, f32[2,1,3,32,512]{4,3,2,1,0:T(8,128)S(1)}, u32[]{:S(2)}, u32[]{:S(2)}) collective-permute-start(f32[2,1,3,32,512]{4,3,2,1,0:T(8,128)S(1)} %shard_map.69), channel_id=1, source_target_pairs={{0,4},{2,6},{4,0},{6,2},{8,12},{10,14},{12,8},{14,10},{16,20},{18,... | collective-permute-start | bytes 1179656 | tf_op jit(solution)/shard_map/ppermute | solution.py:25
  51.0 26.5 %collective-permute-start.6 = (f32[2,2,3,32,512]{4,3,2,1,0:T(8,128)S(1)}, f32[2,2,3,32,512]{4,3,2,1,0:T(8,128)S(1)}, u32[]{:S(2)}, u32[]{:S(2)}) collective-permute-start(f32[2,2,3,32,512]{4,3,2,1,0:T(8,128)S(1)} %get-tuple-element.69), channel_id=1, source_target_pairs={{0,4},{2,6},{4,0},{6,2},{8,12},{10,14},{12,8},{14,10},{16,20},{18,... | collective-permute-start | bytes 2359304 | tf_op jit(solution)/shard_map/ppermute | solution.py:25
  51.5 26.0 %collective-permute-start.10 = (f32[2,2,3,32,512]{4,3,2,1,0:T(8,128)S(1)}, f32[2,2,3,32,512]{4,3,2,1,0:T(8,128)S(1)}, u32[]{:S(2)}, u32[]{:S(2)}) collective-permute-start(f32[2,2,3,32,512]{4,3,2,1,0:T(8,128)S(1)} %get-tuple-element.74), channel_id=1, source_target_pairs={{0,24},{2,26},{4,28},{6,30},{8,16},{10,18},{12,20},{14,22},{16,8},... | collective-permute-start | bytes 2359304 | tf_op jit(solution)/shard_map/ppermute | solution.py:25
  54.0 35.4 %collective-permute-start.11 = (f32[2,2,3,32,512]{4,3,2,1,0:T(8,128)S(1)}, f32[2,2,3,32,512]{4,3,2,1,0:T(8,128)}, u32[]{:S(2)}, u32[]{:S(2)}) collective-permute-start(f32[2,2,3,32,512]{4,3,2,1,0:T(8,128)S(1)} %get-tuple-element.85), channel_id=1, source_target_pairs={{0,8},{2,10},{4,12},{6,14},{8,0},{10,2},{12,4},{14,6},{16,24},{18,... | collective-permute-start | bytes 2359304 | tf_op jit(solution)/shard_map/ppermute | solution.py:25
  54.0 35.4 %collective-permute-start.5 = (f32[3,2,2,32,512]{4,3,2,1,0:T(8,128)S(1)}, f32[3,2,2,32,512]{4,3,2,1,0:T(8,128)S(1)}, u32[]{:S(2)}, u32[]{:S(2)}) collective-permute-start(f32[3,2,2,32,512]{4,3,2,1,0:T(8,128)S(1)} %collective-permute-done.1.refs_2_.refs_3_.refs_12_), channel_id=1, source_target_pairs={{0,1},{1,0},{2,3},{3,2},{4,5},{5,4},{6,7},{7,6},{8,9},{9,8},{10,11... | collective-permute-start | bytes 2359304 | tf_op jit(solution)/shard_map/ppermute | solution.py:25
  62.4 27.2 %collective-permute-start.12 = (f32[12,32,512]{2,1,0:T(8,128)S(1)}, f32[12,32,512]{2,1,0:T(8,128)S(1)}, u32[]{:S(2)}, u32[]{:S(2)}) collective-permute-start(f32[12,32,512]{2,1,0:T(8,128)S(1)} %bitcast.30), channel_id=1, source_target_pairs={{0,1},{1,0},{2,3},{3,2},{4,5},{5,4},{6,7},{7,6},{8,9},{9,8},{10,11... | collective-permute-start | bytes 2359304 | tf_op jit(solution)/shard_map/ppermute | solution.py:25
  90.5 4.6 %collective-permute-start.13 = (f32[2,3,2,64,512]{4,3,2,1,0:T(8,128)S(1)}, f32[2,3,2,64,512]{4,3,2,1,0:T(8,128)S(1)}, u32[]{:S(2)}, u32[]{:S(2)}) collective-permute-start(f32[2,3,2,64,512]{4,3,2,1,0:T(8,128)S(1)} %get-tuple-element.90), channel_id=1, source_target_pairs={{0,2},{2,0},{4,6},{6,4},{8,10},{10,8},{12,14},{14,12},{16,18},{18,... | collective-permute-start | bytes 4718600 | tf_op jit(solution)/shard_map/ppermute | solution.py:25
  90.5 4.5 %collective-permute-start.14 = (f32[2,3,2,32,512]{4,3,2,1,0:T(8,128)S(1)}, f32[2,3,2,32,512]{4,3,2,1,0:T(8,128)S(1)}, u32[]{:S(2)}, u32[]{:S(2)}) collective-permute-start(f32[2,3,2,32,512]{4,3,2,1,0:T(8,128)S(1)} %get-tuple-element.91), channel_id=1, source_target_pairs={{0,2},{2,0},{4,6},{6,4},{8,10},{10,8},{12,14},{14,12},{16,18},{18,... | collective-permute-start | bytes 2359304 | tf_op jit(solution)/shard_map/ppermute | solution.py:25
  91.0 37.4 %collective-permute-start.17 = (f32[2,2,3,32,512]{4,3,2,1,0:T(8,128)S(1)}, f32[2,2,3,32,512]{4,3,2,1,0:T(8,128)}, u32[]{:S(2)}, u32[]{:S(2)}) collective-permute-start(f32[2,2,3,32,512]{4,3,2,1,0:T(8,128)S(1)} %get-tuple-element.84), channel_id=1, source_target_pairs={{0,16},{2,18},{4,20},{6,22},{8,24},{10,26},{12,28},{14,30},{16,0},... | collective-permute-start | bytes 2359304 | tf_op jit(solution)/shard_map/ppermute | solution.py:25
  92.7 35.8 %collective-permute-start.15 = (f32[12,32,512]{2,1,0:T(8,128)S(1)}, f32[12,32,512]{2,1,0:T(8,128)S(1)}, u32[]{:S(2)}, u32[]{:S(2)}) collective-permute-start(f32[12,32,512]{2,1,0:T(8,128)S(1)} %bitcast.33), channel_id=1, source_target_pairs={{0,1},{1,0},{2,3},{3,2},{4,5},{5,4},{6,7},{7,6},{8,9},{9,8},{10,11... | collective-permute-start | bytes 2359304 | tf_op jit(solution)/shard_map/ppermute | solution.py:25
  97.3 31.1 %collective-permute-start.16 = (f32[2,2,3,32,512]{4,3,2,1,0:T(8,128)S(1)}, f32[2,2,3,32,512]{4,3,2,1,0:T(8,128)S(1)}, u32[]{:S(2)}, u32[]{:S(2)}) collective-permute-start(f32[2,2,3,32,512]{4,3,2,1,0:T(8,128)S(1)} %get-tuple-element.98), channel_id=1, source_target_pairs={{0,4},{2,6},{4,0},{6,2},{8,12},{10,14},{12,8},{14,10},{16,20},{18,... | collective-permute-start | bytes 2359304 | tf_op jit(solution)/shard_map/ppermute | solution.py:25
  98.9 35.7 %collective-permute-start.18 = (f32[2,2,3,32,512]{4,3,2,1,0:T(8,128)S(1)}, f32[2,2,3,32,512]{4,3,2,1,0:T(8,128)S(1)}, u32[]{:S(2)}, u32[]{:S(2)}) collective-permute-start(f32[2,2,3,32,512]{4,3,2,1,0:T(8,128)S(1)} %get-tuple-element.101), channel_id=1, source_target_pairs={{0,4},{2,6},{4,0},{6,2},{8,12},{10,14},{12,8},{14,10},{16,20},{18,... | collective-permute-start | bytes 2359304 | tf_op jit(solution)/shard_map/ppermute | solution.py:25
  99.4 53.0 %collective-permute-start.19 = (f32[12,32,512]{2,1,0:T(8,128)}, f32[12,32,512]{2,1,0:T(8,128)}, u32[]{:S(2)}, u32[]{:S(2)}) collective-permute-start(f32[12,32,512]{2,1,0:T(8,128)} %bitcast.11.refs_12_), channel_id=1, source_target_pairs={{0,1},{1,0},{2,3},{3,2},{4,5},{5,4},{6,7},{7,6},{8,9},{9,8},{10,11... | collective-permute-start | bytes 2359304 | tf_op jit(solution)/shard_map/ppermute | solution.py:25
  128.4 24.0 %collective-permute-start.20 = (f32[2,2,3,16,512]{4,3,2,1,0:T(8,128)}, f32[2,2,3,16,512]{4,3,2,1,0:T(8,128)}, u32[]{:S(2)}, u32[]{:S(2)}) collective-permute-start(f32[2,2,3,16,512]{4,3,2,1,0:T(8,128)} %get-tuple-element.105), channel_id=1, source_target_pairs={{0,24},{2,26},{4,28},{6,30},{8,16},{10,18},{12,20},{14,22},{16,8},... | collective-permute-start | bytes 1179656 | tf_op jit(solution)/shard_map/ppermute | solution.py:25
  130.0 34.8 %collective-permute-start.22 = (f32[2,2,3,32,512]{4,3,2,1,0:T(8,128)}, f32[2,2,3,32,512]{4,3,2,1,0:T(8,128)}, u32[]{:S(2)}, u32[]{:S(2)}) collective-permute-start(f32[2,2,3,32,512]{4,3,2,1,0:T(8,128)} %get-tuple-element.110), channel_id=1, source_target_pairs={{0,4},{2,6},{4,0},{6,2},{8,12},{10,14},{12,8},{14,10},{16,20},{18,... | collective-permute-start | bytes 2359304 | tf_op jit(solution)/shard_map/ppermute | solution.py:25
  131.4 13.3 %copy-start.12 = (s32[3,2]{0,1:T(2,128)S(1)}, s32[3,2]{0,1:T(2,128)}, u32[]{:S(2)}) copy-start(s32[3,2]{0,1:T(2,128)} %param.8) | copy-start | bytes 76
  131.4 33.3 %collective-permute-start.23 = (f32[12,32,512]{2,1,0:T(8,128)}, f32[12,32,512]{2,1,0:T(8,128)}, u32[]{:S(2)}, u32[]{:S(2)}) collective-permute-start(f32[12,32,512]{2,1,0:T(8,128)} %bitcast.12.refs_14_), channel_id=1, source_target_pairs={{0,1},{1,0},{2,3},{3,2},{4,5},{5,4},{6,7},{7,6},{8,9},{9,8},{10,11... | collective-permute-start | bytes 2359304 | tf_op jit(solution)/shard_map/ppermute | solution.py:25
  143.2 11.5 %collective-permute-start.21 = (f32[2,2,3,16,512]{4,3,2,1,0:T(8,128)S(1)}, f32[2,2,3,16,512]{4,3,2,1,0:T(8,128)S(1)}, u32[]{:S(2)}, u32[]{:S(2)}) collective-permute-start(f32[2,2,3,16,512]{4,3,2,1,0:T(8,128)S(1)} %get-tuple-element.107), channel_id=1, source_target_pairs={{0,24},{2,26},{4,28},{6,30},{8,16},{10,18},{12,20},{14,22},{16,8},... | collective-permute-start | bytes 1179656 | tf_op jit(solution)/shard_map/ppermute | solution.py:25
  152.4 12.3 %collective-permute-start.24 = (f32[12,16,512]{2,1,0:T(8,128)}, f32[12,16,512]{2,1,0:T(8,128)S(1)}, u32[]{:S(2)}, u32[]{:S(2)}) collective-permute-start(f32[12,16,512]{2,1,0:T(8,128)} %bitcast.13.refs_16_), channel_id=1, source_target_pairs={{0,1},{1,0},{2,3},{3,2},{4,5},{5,4},{6,7},{7,6},{8,9},{9,8},{10,11... | collective-permute-start | bytes 1179656 | tf_op jit(solution)/shard_map/ppermute | solution.py:25
  154.7 17.9 %collective-permute-start.25 = (f32[12,16,512]{2,1,0:T(8,128)S(1)}, f32[12,16,512]{2,1,0:T(8,128)S(1)}, u32[]{:S(2)}, u32[]{:S(2)}) collective-permute-start(f32[12,16,512]{2,1,0:T(8,128)S(1)} %bitcast.36), channel_id=1, source_target_pairs={{0,1},{1,0},{2,3},{3,2},{4,5},{5,4},{6,7},{7,6},{8,9},{9,8},{10,11... | collective-permute-start | bytes 1179656 | tf_op jit(solution)/shard_map/ppermute | solution.py:25
  172.5 20.5 %copy-start.10 = (f32[8,3]{0,1:T(4,128)S(1)}, f32[8,3]{0,1:T(4,128)}, u32[]{:S(2)}) copy-start(f32[8,3]{0,1:T(4,128)} %broadcast_subtract_fusion.1) | copy-start | bytes 292
  180.9 11.8 %all-to-all-start = ((f32[32,3,128]{2,1,0:T(4,128)}), f32[32,3,128]{2,1,0:T(4,128)S(1)}, u32[]{:S(2)}, u32[]{:S(2)}) async-start(f32[32,3,128]{2,1,0:T(4,128)} %bitcast.15), calls=%async_computation | async-start | bytes 131072 | tf_op jit(solution)/shard_map/all_to_all | solution.py:497
  (10 other events, 70.0 us)
